TPU v7x, 32 devices: a whole 2x2x4 slice. The times are simulated.
32 devices in a mesh: seq: 4 (over y, core), dp: 8 (over z, x).
Axes of the slice: x: 2, y: 2, z: 4, core: 2. Of those that a mesh axis runs over, the one named last changes fastest.
Arguments:
- tokens: bfloat16 [16, 1024, 1024], P('dp', 'seq'), may hold values from -6 to 6
- cotangent: bfloat16 [16, 1024, 1024], P('dp', 'seq'), may hold values from -6 to 6
- row_lengths: int32 [16], P('dp'), may hold values from 512 to 1024
- source_lengths: int32 [16], P('dp'), may hold values from 30 to 400
- first_gain: float32 [1024], replicated, may hold values from 0.1 to 1.9
- first_shift: float32 [1024], replicated, may hold values from -2 to 2
- attend_weight: bfloat16 [1024, 3072], replicated, may hold values from -0.25 to 0.25
- attend_bias: float32 [3072], replicated, may hold values from -2 to 2
- output_weight: bfloat16 [1024, 1024], replicated, may hold values from -0.75 to 0.75
- output_bias: float32 [1024], replicated, may hold values from -2 to 2
- second_gain: float32 [1024], replicated, may hold values from 0.1 to 1.9
- second_shift: float32 [1024], replicated, may hold values from -2 to 2
- expand_weight: bfloat16 [1024, 4096], replicated, may hold values from -0.1875 to 0.1875
- expand_bias: float32 [4096], replicated, may hold values from -2 to 2
- contract_weight: bfloat16 [4096, 1024], replicated, may hold values from -0.09375 to 0.09375
- contract_bias: float32 [1024], replicated, may hold values from -2 to 2
- prefix_table: bfloat16 [10, 1024], replicated, may hold values from -6 to 6
- lift_weight: bfloat16 [1024, 512], replicated, may hold values from -0.1875 to 0.1875
- lift_bias: float32 [512], replicated, may hold values from -2 to 2
- fan_weight: bfloat16 [512, 2048], replicated, may hold values from -0.375 to 0.375
- fan_bias: float32 [2048], replicated, may hold values from -2 to 2
Outputs:
- activations: bfloat16 [16, 1024, 1024], P('dp', 'seq')
- input_grad: float32 [16, 1024, 1024], P('dp', 'seq')
- grad_table: float32 [10, 1024], replicated
- grad_lift: float32 [1024, 512], replicated
- grad_liftbias: float32 [512], replicated
- grad_fan: float32 [512, 2048], replicated
- grad_fanbias: float32 [2048], replicated
All inputs are finite; a program needn't handle non-finite values.
Results may differ from a plain program's by a relative error of at most 0.025.
Values may be sent and summed in bfloat16 or wider, within the bound.
No kernel may reach another device: no remote copies, remote signals or barrier semaphores. Data moves between devices by JAX's collectives and lax.ppermute only.
A program may use at most 320 MiB of HBM per device.

v0:
```python
import jax
import jax.numpy as jnp
from jax import lax
from jax.sharding import PartitionSpec as P

D = 1024
HEADS = 16
HEAD_DIM = 64
PREFIX = 10


best_precision = lax.Precision.HIGHEST


def layer_norm(values, norm_gain, norm_shift):
    centred = values - jnp.mean(values, axis=-1, keepdims=True)
    variance = jnp.mean(centred * centred, axis=-1, keepdims=True)
    return centred * lax.rsqrt(variance + 1e-05) * norm_gain + norm_shift


def gelu_tanh(values):
    return jax.nn.gelu(values, approximate=True)


def block_forward(tokens, row_lengths, frozen, prefix_keyval, again):
    (
        first_gain,
        first_shift,
        attend_weight,
        attend_bias,
        output_weight,
        output_bias,
        second_gain,
        second_shift,
        expand_weight,
        expand_bias,
        contract_weight,
        contract_bias,
    ) = frozen
    row_count = tokens.shape[0]
    tok_count = tokens.shape[1]
    inputs = tokens.astype(jnp.float32)
    normed = layer_norm(inputs, first_gain, first_shift).astype(jnp.bfloat16)
    project = jnp.dot(normed, attend_weight, preferred_element_type=jnp.float32) + attend_bias
    queries = project[..., :D].astype(jnp.bfloat16).reshape(row_count, tok_count, HEADS, HEAD_DIM)
    local_keyval = project[..., D:].astype(jnp.bfloat16)
    if again:
        row_keyval = lax.all_gather(local_keyval, "seq", axis=1, tiled=True)
    else:
        row_keyval = lax.all_gather(local_keyval, "seq", axis=1, tiled=True)
    seq_total = row_keyval.shape[1]
    row_keys = row_keyval[..., :D].reshape(row_count, seq_total, HEADS, HEAD_DIM)
    row_values = row_keyval[..., D:].reshape(row_count, seq_total, HEADS, HEAD_DIM)
    prefix_keys = prefix_keyval[:, :D].reshape(PREFIX, HEADS, HEAD_DIM)
    prefix_values = prefix_keyval[:, D:].reshape(PREFIX, HEADS, HEAD_DIM)
    scores = (
        jnp.einsum("rqhd,rkhd->rhqk", queries, row_keys, preferred_element_type=jnp.float32) * 0.125
    )
    prefix_scores = (
        jnp.einsum("rqhd,phd->rhqp", queries, prefix_keys, preferred_element_type=jnp.float32)
        * 0.125
    )
    query_places = lax.axis_index("seq") * tok_count + jnp.arange(tok_count)
    key_places = jnp.arange(seq_total)
    visible = (key_places[None, None, :] <= query_places[None, :, None]) & (
        key_places[None, None, :] < row_lengths[:, None, None]
    )
    scores = jnp.where(visible[:, None], scores, -jnp.inf)
    highest = jnp.maximum(
        jnp.max(scores, axis=-1, keepdims=True), jnp.max(prefix_scores, axis=-1, keepdims=True)
    )
    denominator = jnp.sum(jnp.exp(scores - highest), axis=-1, keepdims=True) + jnp.sum(
        jnp.exp(prefix_scores - highest), axis=-1, keepdims=True
    )
    log_total = highest + jnp.log(denominator)
    weights = jnp.exp(scores - log_total)
    prefix_weights = jnp.exp(prefix_scores - log_total)
    rounded = weights.astype(jnp.bfloat16)
    prefix_rounded = prefix_weights.astype(jnp.bfloat16)
    attended = jnp.einsum(
        "rhqk,rkhd->rqhd", rounded, row_values, preferred_element_type=jnp.float32
    )
    attended = attended + jnp.einsum(
        "rhqp,phd->rqhd", prefix_rounded, prefix_values, preferred_element_type=jnp.float32
    )
    mixed_heads = attended.reshape(row_count, tok_count, D).astype(jnp.bfloat16)
    residual = (
        inputs
        + jnp.dot(mixed_heads, output_weight, preferred_element_type=jnp.float32)
        + output_bias
    )
    normed_two = layer_norm(residual, second_gain, second_shift).astype(jnp.bfloat16)
    expanded = jnp.dot(normed_two, expand_weight, preferred_element_type=jnp.float32) + expand_bias
    activated = gelu_tanh(expanded).astype(jnp.bfloat16)
    result = (
        residual
        + jnp.dot(activated, contract_weight, preferred_element_type=jnp.float32)
        + contract_bias
    )
    return (
        inputs,
        queries,
        row_keys,
        row_values,
        prefix_keys,
        prefix_values,
        weights,
        prefix_weights,
        rounded,
        prefix_rounded,
        residual,
        expanded,
        result,
        log_total,
    )


def prefix_grads(prefix_grad, prefix_table, lift_weight, fan_weight, lifted, lifted_low):
    grad_fanbias = jnp.sum(prefix_grad, axis=0)
    grad_fan = jnp.dot(lifted_low.astype(jnp.float32).T, prefix_grad, precision=best_precision)
    grad_lifted = jnp.dot(
        prefix_grad, fan_weight.astype(jnp.float32).T, precision=best_precision
    ) * (1.0 - lifted * lifted)
    grad_liftbias = jnp.sum(grad_lifted, axis=0)
    grad_lift = jnp.dot(prefix_table.astype(jnp.float32).T, grad_lifted, precision=best_precision)
    grad_table = jnp.dot(grad_lifted, lift_weight.astype(jnp.float32).T, precision=best_precision)
    return (grad_table, grad_lift, grad_liftbias, grad_fan, grad_fanbias)


def per_device(
    tokens,
    cotangent,
    row_lengths,
    source_lengths,
    first_gain,
    first_shift,
    attend_weight,
    attend_bias,
    output_weight,
    output_bias,
    second_gain,
    second_shift,
    expand_weight,
    expand_bias,
    contract_weight,
    contract_bias,
    prefix_table,
    lift_weight,
    lift_bias,
    fan_weight,
    fan_bias,
):
    frozen = (
        first_gain,
        first_shift,
        attend_weight,
        attend_bias,
        output_weight,
        output_bias,
        second_gain,
        second_shift,
        expand_weight,
        expand_bias,
        contract_weight,
        contract_bias,
    )
    lifted = jnp.tanh(
        jnp.dot(prefix_table, lift_weight, preferred_element_type=jnp.float32) + lift_bias
    )
    lifted_low = lifted.astype(jnp.bfloat16)
    prefix_keyval = (
        jnp.dot(lifted_low, fan_weight, preferred_element_type=jnp.float32) + fan_bias
    ).astype(jnp.bfloat16)
    state = block_forward(tokens, row_lengths, frozen, prefix_keyval, False)
    activations = state[12].astype(jnp.bfloat16)
    again_tokens = lax.optimization_barrier((tokens, activations))[0]
    state = block_forward(again_tokens, row_lengths, frozen, prefix_keyval, True)
    (
        inputs,
        queries,
        row_keys,
        row_values,
        prefix_keys,
        prefix_values,
        weights,
        prefix_weights,
        rounded,
        prefix_rounded,
        residual,
        expanded,
        result,
        log_total,
    ) = state
    row_count = tokens.shape[0]
    tok_count = tokens.shape[1]
    places = lax.axis_index("seq") * tok_count + jnp.arange(tok_count)
    target = (places[None, :] >= source_lengths[:, None]) & (places[None, :] < row_lengths[:, None])
    grad_out = jnp.where(target[..., None], cotangent, jnp.zeros_like(cotangent))
    grad_hidden = jnp.einsum(
        "rcd,fd->rcf", grad_out, contract_weight, preferred_element_type=jnp.float32
    )
    _, gelu_back = jax.vjp(gelu_tanh, expanded)
    grad_expand = gelu_back(grad_hidden)[0].astype(jnp.bfloat16)
    grad_normed = jnp.einsum(
        "rcf,df->rcd", grad_expand, expand_weight, preferred_element_type=jnp.float32
    )
    _, second_back = jax.vjp(lambda values: layer_norm(values, second_gain, second_shift), residual)
    grad_residual = grad_out.astype(jnp.float32) + second_back(grad_normed)[0]
    grad_mixed = jnp.einsum(
        "rcd,ed->rce",
        grad_residual.astype(jnp.bfloat16),
        output_weight,
        preferred_element_type=jnp.float32,
    )
    grad_heads = grad_mixed.astype(jnp.bfloat16).reshape(row_count, tok_count, HEADS, HEAD_DIM)
    grad_weights = jnp.einsum(
        "rqhd,rkhd->rhqk", grad_heads, row_values, preferred_element_type=jnp.float32
    )
    grad_preweights = jnp.einsum(
        "rqhd,phd->rhqp", grad_heads, prefix_values, preferred_element_type=jnp.float32
    )
    inner_sum = jnp.sum(weights * grad_weights, axis=-1, keepdims=True) + jnp.sum(
        prefix_weights * grad_preweights, axis=-1, keepdims=True
    )
    grad_scores = (weights * (grad_weights - inner_sum)).astype(jnp.bfloat16)
    grad_prescores = (prefix_weights * (grad_preweights - inner_sum)).astype(jnp.bfloat16)
    grad_queries = jnp.einsum(
        "rhqk,rkhd->rqhd", grad_scores, row_keys, preferred_element_type=jnp.float32
    )
    grad_queries = (
        grad_queries
        + jnp.einsum(
            "rhqp,phd->rqhd", grad_prescores, prefix_keys, preferred_element_type=jnp.float32
        )
    ) * 0.125
    grad_keys = (
        jnp.einsum("rhqk,rqhd->krhd", grad_scores, queries, preferred_element_type=jnp.float32)
        * 0.125
    )
    grad_values = jnp.einsum(
        "rhqk,rqhd->krhd", rounded, grad_heads, preferred_element_type=jnp.float32
    )
    owned = lax.psum_scatter(
        jnp.concatenate(
            [
                grad_keys.reshape(tok_count * lax.axis_size("seq"), row_count, D),
                grad_values.reshape(tok_count * lax.axis_size("seq"), row_count, D),
            ],
            axis=-1,
        ).astype(jnp.bfloat16),
        "seq",
        scatter_dimension=0,
        tiled=True,
    ).astype(jnp.float32)
    grad_owned = jnp.transpose(owned, (1, 0, 2)).astype(jnp.bfloat16)
    grad_prekeys = (
        jnp.einsum("rhqp,rqhd->phd", grad_prescores, queries, preferred_element_type=jnp.float32)
        * 0.125
    )
    grad_prevalues = jnp.einsum(
        "rhqp,rqhd->phd", prefix_rounded, grad_heads, preferred_element_type=jnp.float32
    )
    prefix_grad = jnp.concatenate(
        [grad_prekeys.reshape(PREFIX, D), grad_prevalues.reshape(PREFIX, D)], axis=-1
    )
    grad_project = jnp.concatenate(
        [grad_queries.reshape(row_count, tok_count, D).astype(jnp.bfloat16), grad_owned], axis=-1
    )
    grad_first = jnp.einsum(
        "rcf,df->rcd", grad_project, attend_weight, preferred_element_type=jnp.float32
    )
    _, first_back = jax.vjp(lambda values: layer_norm(values, first_gain, first_shift), inputs)
    input_grad = grad_residual + first_back(grad_first)[0]
    grad_table, grad_lift, grad_liftbias, grad_fan, grad_fanbias = prefix_grads(
        prefix_grad, prefix_table, lift_weight, fan_weight, lifted, lifted_low
    )
    grad_table, grad_lift, grad_liftbias, grad_fan, grad_fanbias = lax.psum(
        (grad_table, grad_lift, grad_liftbias, grad_fan, grad_fanbias), ("seq", "dp")
    )
    return (activations, input_grad, grad_table, grad_lift, grad_liftbias, grad_fan, grad_fanbias)


def solution(mesh):
    return jax.shard_map(
        per_device,
        mesh=mesh,
        in_specs=(
            P("dp", "seq", None),
            P("dp", "seq", None),
            P("dp"),
            P("dp"),
            P(),
            P(),
            P(),
            P(),
            P(),
            P(),
            P(),
            P(),
            P(),
            P(),
            P(),
            P(),
            P(),
            P(),
            P(),
            P(),
            P(),
        ),
        out_specs=(P("dp", "seq", None), P("dp", "seq", None), P(), P(), P(), P(), P()),
        check_vma=False,
    )
```

profile of v0, /device:TPU:0, one launch (start us, length us, event | category | flops | bytes accessed | tf_op | source)
XLA Modules:
  0.0 669.3 jit_solution(5564932534469927278)
XLA Ops:
  10.5 6.6 add_convert_fusion.1
  20.5 2.3 slice.48
  28.4 53.0 %all-gather.3.cloned.1.call-done = bf16[2,1024,2048]{2,1,0:T(8,128)(2,1)} async-done(((bf16[2,256,2048]{2,1,0:T(8,128)(2,1)}), bf16[2,1024,2048]{2,1,0:T(8,128)(2,1)}) %all-gather.3.cloned.1.call-update) | async-done | bytes 8388624 | tf_op jit(solution)/shard_map/all_gather | solution.py:50
  81.4 6.0 fusion.174
  87.4 6.2 copy.171
  93.6 6.2 copy.173
  99.8 15.9 %fusion = (f32[2,16,256]{2,1,0:T(8,128)S(1)}, f32[2,16,256,1024]{3,2,1,0:T(8,128)}) fusion(pred[2,256,1024]{2,1,0:T(8,128)(4,1)S(1)} %broadcast_and_fusion, bf16[2,256,16,64]{1,3,2,0:T(8,128)(2,1)} %bitcast.197, bf16[2,1024,16,64]{1,3,2,0:T(8,128)(2,1)} %bitcast.195), kind=kOutput, calls=%fused_computation.8 | convolution fusion | flops 1098899456 | bytes 39354368 | tf_op jit(solution)/shard_map/rqhd,rkhd->rhqk/dot_general | solution.py:57
  116.0 14.9 %exponential_reduce_fusion.1 = f32[2,16,256]{2,1,0:T(8,128)S(1)} fusion(f32[2,16,256,1024]{3,2,1,0:T(8,128)} %get-tuple-element.60, f32[2,16,256]{2,1,0:T(8,128)S(1)} %max.22, pred[2,256,1024]{2,1,0:T(8,128)(4,1)S(1)} %broadcast_and_fusion), kind=kLoop, calls=%fused_computation.6 | loop fusion | flops 33546240 | bytes 34144256 | tf_op jit(solution)/shard_map/reduce_sum | solution.py:72
  132.9 17.7 %fusion.74 = bf16[2,256,16,64]{1,3,2,0:T(8,128)(2,1)} fusion(f32[16,64,2,256]{3,1,0,2:T(8,128)} %fusion.137, bf16[2,1024,16,64]{1,3,2,0:T(8,128)(2,1)} %bitcast.198, f32[2,16,256,1024]{3,2,1,0:T(8,128)} %get-tuple-element.60, f32[2,16,256]{2,1,0:T(8,128)S(1)} %log_add_fusion.1, pred[2,256,1024]{2,1,0:T(8,128)(4,1)} %copy-done.2), kind=kOutput, calls=%fused_computation.94 | convolution fusion | flops 1108344832 | bytes 41451520 | tf_op jit(solution)/shard_map/rhqk,rkhd->rqhd/dot_general | solution.py:80
  150.8 2.7 fusion.176
  153.9 10.4 %fusion.19 = bf16[2,256,4096]{2,1,0:T(8,128)(2,1)S(1)} fusion(bf16[1024,4096]{1,0:T(8,128)(2,1)} %param.33, f32[4096]{0:T(1024)S(1)} %copy-done.45, f32[2,256,1024]{2,1,0:T(8,128)S(1)} %get-tuple-element.62, f32[1024]{0:T(1024)S(1)} %copy-done.49, f32[1024]{0:T(1024)S(1)} %copy-done.38, f32[2,256]{1,0:T(2,128)S(1)} %add_rsqrt_fusion, ...), kind=kOutput, calls=%fused_computation.30 | convolution fusion | flops 4318560256 | bytes 14708736 | tf_op jit(solution)/shard_map/dot_general | solution.py:93
  164.5 5.5 add_convert_fusion.3
  170.7 4.0 add_convert_fusion
  178.1 12.7 %fusion.20 = f32[2,256,4096]{2,1,0:T(8,128)} fusion(bf16[4096,1024]{1,0:T(8,128)(2,1)} %param.35, bf16[2,256,1024]{2,1,0:T(8,128)(2,1)} %param.22, pred[2,256]{1,0:T(4,128)(4,1)S(1)} %compare_and_fusion), kind=kOutput, calls=%fused_computation.32 | convolution fusion | flops 4295491584 | bytes 17826304 | tf_op jit(solution)/shard_map/rcd,fd->rcf/dot_general | solution.py:199
  190.8 2.3 slice.54
  193.1 2.4 copy.185
  197.2 39.1 %all-gather.5.cloned.1.call-done = bf16[2,1024,2048]{2,1,0:T(8,128)(2,1)} async-done(((bf16[2,256,2048]{2,1,0:T(8,128)(2,1)}), bf16[2,1024,2048]{2,1,0:T(8,128)(2,1)}) %all-gather.5.cloned.1.call-update) | async-done | bytes 8388624 | tf_op jit(solution)/shard_map/all_gather | solution.py:48
  236.4 6.0 fusion.173
  242.4 6.2 copy.186
  248.6 6.2 copy.184
  254.8 15.9 %fusion.1 = (f32[2,16,256]{2,1,0:T(8,128)S(1)}, f32[2,16,256,1024]{3,2,1,0:T(8,128)}) fusion(pred[2,256,1024]{2,1,0:T(8,128)(4,1)} %copy-done.2, bf16[2,256,16,64]{1,3,2,0:T(8,128)(2,1)} %bitcast.185, bf16[2,1024,16,64]{1,3,2,0:T(8,128)(2,1)} %bitcast.182), kind=kOutput, calls=%fused_computation.9 | convolution fusion | flops 1098899456 | bytes 39354368 | tf_op jit(solution)/shard_map/rqhd,rkhd->rhqk/dot_general | solution.py:57
  270.8 14.9 %exponential_reduce_fusion = f32[2,16,256]{2,1,0:T(8,128)S(1)} fusion(f32[2,16,256,1024]{3,2,1,0:T(8,128)} %get-tuple-element.64, f32[2,16,256]{2,1,0:T(8,128)S(1)} %max.23, pred[2,256,1024]{2,1,0:T(8,128)(4,1)S(1)} %copy-done.3), kind=kLoop, calls=%fused_computation.3 | loop fusion | flops 33546240 | bytes 34144256 | tf_op jit(solution)/shard_map/reduce_sum | solution.py:72
  286.4 17.0 %fusion.141 = f32[2,16,64,256]{3,2,1,0:T(8,128)} fusion(bf16[2,1024,16,64]{1,3,2,0:T(8,128)(2,1)} %bitcast.188, f32[2,16,256,1024]{3,2,1,0:T(8,128)} %get-tuple-element.64, f32[2,16,256]{2,1,0:T(8,128)S(1)} %log_add_fusion, pred[2,256,1024]{2,1,0:T(8,128)(4,1)} %copy-done.2), kind=kOutput, calls=%fused_computation.169 | convolution fusion | flops 1107296256 | bytes 40402944 | tf_op jit(solution)/shard_map/rhqk,rkhd->rqhd/dot_general | solution.py:80
  303.4 2.2 fusion.67
  309.2 23.7 %multiply_reduce_fusion.1 = (f32[2,256]{1,0:T(2,128)}, f32[2,256,1024]{2,1,0:T(8,128)}) fusion(f32[2,256,1024]{2,1,0:T(8,128)} %copy-done.4, f32[2,256]{1,0:T(2,128)S(1)} %broadcast_multiply_fusion, f32[1024]{0:T(1024)} %param.31, bf16[1024,4096]{1,0:T(8,128)(2,1)} %param.33, f32[2,256,4096]{2,1,0:T(8,128)} %fusion.20, f32[4096]{0:T(1024)} %param.34, ...), kind=kOutput, calls=%fused_computation.97 | convolution fusion | flops 8638693376 | bytes 21002240 | tf_op jit(solution)/shard_map/rcf,df->rcd/dot_general | solution.py:204
  333.7 2.9 fusion.172
  337.9 2.4 fusion.77
  340.3 2.2 copy.197
  344.2 27.5 %multiply_reduce_fusion = (f32[2,16,256]{2,1,0:T(8,128)}, f32[2,16,256,1024]{3,2,1,0:T(8,128)}) fusion(f32[2,16,256,1024]{3,2,1,0:T(8,128)} %get-tuple-element.64, f32[2,16,256]{2,1,0:T(8,128)S(1)} %log_add_fusion, pred[2,256,1024]{2,1,0:T(8,128)(4,1)} %copy-done.2, bf16[2,256,16,64]{1,3,2,0:T(8,128)(2,1)} %bitcast.192, bf16[2,1024,16,64]{1,3,2,0:T(8,128)(2,1)} %bitcast.189), kind=kOutput, calls=%fused_computation.1 | convolution fusion | flops 1115676672 | bytes 72941568 | tf_op jit(solution)/shard_map/rqhd,rkhd->rhqk/dot_general | solution.py:216
  380.5 3.3 fusion.180
  383.9 3.8 fusion.152
  387.6 28.0 %multiply_convert_fusion = bf16[2,16,256,1024]{3,2,1,0:T(8,128)(2,1)} fusion(f32[2,16,256,1024]{3,2,1,0:T(8,128)} %get-tuple-element.70, f32[2,16,256,1024]{3,2,1,0:T(8,128)} %get-tuple-element.64, f32[2,16,256]{2,1,0:T(8,128)S(1)} %copy-done.23, f32[2,16,256]{2,1,0:T(8,128)S(1)} %log_add_fusion, pred[2,256,1024]{2,1,0:T(8,128)(4,1)} %copy-done.2), kind=kLoop, calls=%fused_computation | loop fusion | flops 50331648 | bytes 84475904 | tf_op jit(solution)/shard_map/convert_element_type | solution.py:225
  415.6 2.3 convolution_bitcast_fusion
  418.0 18.1 %convolution_convert_fusion = bf16[2,16,64,1024]{3,2,1,0:T(8,128)(2,1)} fusion(bf16[2,256,16,64]{1,3,2,0:T(8,128)(2,1)} %bitcast.194, f32[2,16,256,1024]{3,2,1,0:T(8,128)} %get-tuple-element.64, f32[2,16,256]{2,1,0:T(8,128)S(1)} %log_add_fusion, pred[2,256,1024]{2,1,0:T(8,128)(4,1)} %copy-done.2), kind=kOutput, calls=%fused_computation.66 | convolution fusion | flops 1109393408 | bytes 39354368 | tf_op jit(solution)/shard_map/rhqk,rqhd->krhd/dot_general | solution.py:240
  436.1 6.3 copy.206
  442.5 11.3 %multiply_convert_fusion.1 = bf16[2,16,64,1024]{3,2,1,0:T(8,128)(2,1)} fusion(bf16[2,256,16,64]{1,3,2,0:T(8,128)(2,1)} %bitcast.187, bf16[2,16,256,1024]{3,2,1,0:T(8,128)(2,1)} %multiply_convert_fusion), kind=kOutput, calls=%fused_computation.42 | convolution fusion | flops 1077936128 | bytes 22020096 | tf_op jit(solution)/shard_map/rhqk,rqhd->krhd/dot_general | solution.py:237
  453.8 6.5 copy.205
  460.2 8.5 %pad_maximum_fusion = bf16[1024,2,2048]{2,0,1:T(8,128)(2,1)} fusion(bf16[1024,2,1024]{2,0,1:T(8,128)(2,1)} %copy.206, bf16[1024,2,1024]{2,0,1:T(8,128)(2,1)} %copy.205), kind=kLoop, calls=%fused_computation.31 | loop fusion | flops 16777216 | bytes 16777216 | tf_op jit(solution)/shard_map/concatenate | solution.py:244
  468.8 13.8 %fusion.181 = f32[2,16,64,256]{3,2,1,0:T(8,128)} fusion(bf16[2,1024,16,64]{1,3,2,0:T(8,128)(2,1)} %bitcast.183, bf16[2,16,256,1024]{3,2,1,0:T(8,128)(2,1)} %multiply_convert_fusion), kind=kOutput, calls=%fused_computation.225 | convolution fusion | flops 1073741824 | bytes 23068672 | tf_op jit(solution)/shard_map/rhqk,rkhd->rqhd/dot_general | solution.py:227
  482.6 3.1 fusion.66
  485.7 2.3 copy.207
  488.0 2.1 fusion.182
  490.1 40.9 %all-reduce = (f32[10,1024]{1,0:T(8,128)}, f32[512]{0:T(512)}, f32[2048]{0:T(1024)}) all-reduce(f32[10,1024]{1,0:T(8,128)S(1)} %fusion.182, f32[512]{0:T(512)S(1)} %get-tuple-element.73, f32[2048]{0:T(1024)S(1)} %reduce_sum.231), channel_id=1, replica_groups=mesh['seq'=4,'dp'=8] {'seq','dp'}, use_global_device_ids=true, to_apply=%region_23.24 | all-reduce | flops 12800 | bytes 102400 | tf_op jit(solution)/shard_map/psum | solution.py:277
  531.0 43.9 %all-reduce.4.cloned.1.call-done = (f32[1024,512]{0,1:T(8,128)}, f32[512,2048]{1,0:T(8,128)}) async-done(((f32[1024,512]{0,1:T(8,128)}, f32[512,2048]{1,0:T(8,128)}), (f32[1024,512]{0,1:T(8,128)}, f32[512,2048]{1,0:T(8,128)})) %all-reduce.4.cloned.1.call-update) | async-done | bytes 6291472 | tf_op jit(solution)/shard_map/psum | solution.py:277
  574.9 2.9 copy.212
  577.8 71.4 %reduce-scatter.2.cloned.1.call-done = bf16[256,2,2048]{2,0,1:T(8,128)(2,1)} async-done(((bf16[1024,2,2048]{2,0,1:T(8,128)(2,1)}), bf16[256,2,2048]{2,0,1:T(8,128)(2,1)}) %reduce-scatter.2.cloned.1.call-update) | async-done | bytes 2097168 | tf_op jit(solution)/shard_map/reduce_scatter | solution.py:243
  649.3 6.7 %fusion.63 = (f32[2,256]{1,0:T(2,128)S(1)}, f32[2,256,1024]{2,1,0:T(8,128)S(1)}) fusion(bf16[2,256,1024]{2,1,0:T(8,128)(2,1)S(1)} %copy-done.1, f32[2,256]{1,0:T(2,128)S(1)} %copy-done.30, f32[1024]{0:T(1024)S(1)} %copy-done.36, bf16[1024,3072]{1,0:T(8,128)(2,1)} %param.27, bf16[2,256,2048]{2,1,0:T(8,128)(2,1)} %bitcast.210, bf16[2,256,1024]{2,1,0:T(8,128)(2,1)} %copy.207), kind=kOutput, calls=%fused_computation.80 | convolution fusion | flops 3230137856 | bytes 12591104 | tf_op jit(solution)/shard_map/rcf,df->rcd/dot_general | solution.py:269
  657.6 2.1 add_add_fusion.2
  (178 shorter events, 42.1 us)
Async XLA Ops:
  7.2 143.5 %copy-start = (bf16[1024,1024]{1,0:T(8,128)(2,1)S(1)}, bf16[1024,1024]{1,0:T(8,128)(2,1)}, u32[]{:S(2)}) copy-start(bf16[1024,1024]{1,0:T(8,128)(2,1)} %param.29) | copy-start | bytes 6291460
  7.2 74.2 %all-gather.3.cloned.1.call-start = ((), (), s32[]{:S(2)}) async-start(), calls=%async_computation.1 | async-start | bytes 10485760 | tf_op jit(solution)/shard_map/all_gather | solution.py:50
  18.7 4.0 copy-start.11
  18.7 4.0 copy-start.26
  18.7 4.0 copy-start.42
  18.7 4.3 copy-start.37
  20.3 216.1 %all-gather.5.cloned.1.call-start = ((), (), s32[]{:S(2)}) async-start(), calls=%async_computation.2 | async-start | bytes 10485760 | tf_op jit(solution)/shard_map/all_gather | solution.py:48
  22.8 4.5 copy-start.43
  23.0 2.0 copy-start.20
  25.3 170.3 %copy-start.16 = (bf16[10,16,64]{2,1,0:T(8,128)(2,1)}, bf16[10,16,64]{2,1,0:T(8,128)(2,1)S(1)}, u32[]{:S(2)}) copy-start(bf16[10,16,64]{2,1,0:T(8,128)(2,1)S(1)} %reshape.304) | copy-start | bytes 61444
  28.4 87.6 %copy-start.2 = (pred[2,256,1024]{2,1,0:T(8,128)(4,1)}, pred[2,256,1024]{2,1,0:T(8,128)(4,1)S(1)}, u32[]{:S(2)}) copy-start(pred[2,256,1024]{2,1,0:T(8,128)(4,1)S(1)} %broadcast_and_fusion) | copy-start | bytes 1572868
  99.8 15.9 %copy-start.7 = (f32[16,10,2,256]{3,1,2,0:T(8,128)S(1)}, f32[16,10,2,256]{3,1,2,0:T(8,128)}, u32[]{:S(2)}) copy-start(f32[16,10,2,256]{3,1,2,0:T(8,128)} %copy-done.6) | copy-start | bytes 983044
  132.9 17.8 %copy-start.1 = (bf16[2,256,1024]{2,1,0:T(8,128)(2,1)S(1)}, bf16[2,256,1024]{2,1,0:T(8,128)(2,1)}, u32[]{:S(2)}) copy-start(bf16[2,256,1024]{2,1,0:T(8,128)(2,1)} %param.21) | copy-start | bytes 3145732
  132.9 17.8 %copy-start.28 = (f32[1024]{0:T(1024)S(1)}, f32[1024]{0:T(1024)}, u32[]{:S(2)}) copy-start(f32[1024]{0:T(1024)} %param.30) | copy-start | bytes 12292
  150.7 3.2 copy-start.38
  150.7 3.2 copy-start.45
  150.7 3.2 copy-start.49
  150.7 13.6 %slice-start = ((s8[8388608]{0:T(1024)(128)(4,1)}), s8[4194304]{0:T(1024)(128)(4,1)S(1)}, s32[]{:S(2)}) async-start(s8[8388608]{0:T(1024)(128)(4,1)} %bitcast.206), calls=%async_computation.5 | async-start | bytes 8388608
  150.7 19.9 %slice-start.2 = ((s8[6291456]{0:T(1024)(128)(4,1)}), s8[4194304]{0:T(1024)(128)(4,1)S(1)}, s32[]{:S(2)}) async-start(s8[6291456]{0:T(1024)(128)(4,1)} %bitcast.208), calls=%async_computation.7 | async-start | bytes 8388608
  153.9 10.5 %slice-start.1 = ((s8[8388608]{0:T(1024)(128)(4,1)}), s8[4194304]{0:T(1024)(128)(4,1)S(1)}, s32[]{:S(2)}) async-start(s8[8388608]{0:T(1024)(128)(4,1)} %bitcast.206), calls=%async_computation.6 | async-start | bytes 8388608
  153.9 10.5 %copy-start.47 = (f32[1024]{0:T(1024)S(1)}, f32[1024]{0:T(1024)}, u32[]{:S(2)}) copy-start(f32[1024]{0:T(1024)} %param.36) | copy-start | bytes 12292
  153.9 16.7 %slice-start.3 = ((s8[6291456]{0:T(1024)(128)(4,1)}), s8[2097152]{0:T(1024)(128)(4,1)S(1)}, s32[]{:S(2)}) async-start(s8[6291456]{0:T(1024)(128)(4,1)} %bitcast.208), calls=%async_computation.8 | async-start | bytes 4194304
  164.4 6.3 copy-start.35
  164.4 6.3 copy-start.46
  164.4 6.2 copy-start.48
  170.2 4.5 copy-start.29
  170.6 4.1 copy-start.31
  170.7 4.0 copy-start.33
  178.0 397.0 %all-reduce.4.cloned.1.call-start = ((), (), s32[]{:S(2)}) async-start(), calls=%async_computation.4 | async-start | bytes 12582912 | tf_op jit(solution)/shard_map/psum | solution.py:277
  178.1 12.7 %copy-start.39 = (pred[2,256]{1,0:T(4,128)(4,1)}, pred[2,256]{1,0:T(4,128)(4,1)S(1)}, u32[]{:S(2)}) copy-start(pred[2,256]{1,0:T(4,128)(4,1)S(1)} %compare_and_fusion) | copy-start | bytes 1540
  254.8 16.0 %copy-start.3 = (pred[2,256,1024]{2,1,0:T(8,128)(4,1)S(1)}, pred[2,256,1024]{2,1,0:T(8,128)(4,1)}, u32[]{:S(2)}) copy-start(pred[2,256,1024]{2,1,0:T(8,128)(4,1)} %copy-done.2) | copy-start | bytes 1572868
  332.9 5.0 copy-start.18
  332.9 5.0 copy-start.40
  375.4 8.4 %copy-start.21 = (f32[10,512]{1,0:T(8,128)S(1)}, f32[10,512]{1,0:T(8,128)}, u32[]{:S(2)}) copy-start(f32[10,512]{1,0:T(8,128)} %copy-done.20) | copy-start | bytes 61444
  377.9 9.7 %copy-start.23 = (f32[2,16,256]{2,1,0:T(8,128)S(1)}, f32[2,16,256]{2,1,0:T(8,128)}, u32[]{:S(2)}) copy-start(f32[2,16,256]{2,1,0:T(8,128)} %copy-done.22) | copy-start | bytes 98308
  383.9 31.8 %copy-start.24 = (f32[10,512]{1,0:T(8,128)}, f32[10,512]{1,0:T(8,128)S(1)}, u32[]{:S(2)}) copy-start(f32[10,512]{1,0:T(8,128)S(1)} %get-tuple-element.74) | copy-start | bytes 61444
  387.6 28.0 %copy-start.27 = (bf16[10,1024]{1,0:T(8,128)(2,1)S(1)}, bf16[10,1024]{1,0:T(8,128)(2,1)}, u32[]{:S(2)}) copy-start(bf16[10,1024]{1,0:T(8,128)(2,1)} %param.37) | copy-start | bytes 61444
  418.0 231.2 %reduce-scatter.2.cloned.1.call-start = ((), (), s32[]{:S(2)}) async-start(), calls=%async_computation.3 | async-start | bytes 10485760 | tf_op jit(solution)/shard_map/reduce_scatter | solution.py:243
  468.8 13.8 %copy-start.15 = (bf16[2,16,256,10]{2,1,3,0:T(8,128)(2,1)S(1)}, bf16[2,16,256,10]{2,1,3,0:T(8,128)(2,1)}, u32[]{:S(2)}) copy-start(bf16[2,16,256,10]{2,1,3,0:T(8,128)(2,1)} %copy-done.14) | copy-start | bytes 491524
  468.8 13.8 %copy-start.17 = (bf16[10,16,64]{2,1,0:T(8,128)(2,1)S(1)}, bf16[10,16,64]{2,1,0:T(8,128)(2,1)}, u32[]{:S(2)}) copy-start(bf16[10,16,64]{2,1,0:T(8,128)(2,1)} %copy-done.16) | copy-start | bytes 61444
  482.6 5.4 copy-start.25
  485.7 163.5 %copy-start.30 = (f32[2,256]{1,0:T(2,128)S(1)}, f32[2,256]{1,0:T(2,128)}, u32[]{:S(2)}) copy-start(f32[2,256]{1,0:T(2,128)} %copy-done.29) | copy-start | bytes 6148
  485.7 163.5 %copy-start.36 = (f32[1024]{0:T(1024)S(1)}, f32[1024]{0:T(1024)}, u32[]{:S(2)}) copy-start(f32[1024]{0:T(1024)} %param.25) | copy-start | bytes 12292
  649.2 6.8 %copy-start.32 = (f32[2,256]{1,0:T(2,128)S(1)}, f32[2,256]{1,0:T(2,128)}, u32[]{:S(2)}) copy-start(f32[2,256]{1,0:T(2,128)} %copy-done.31) | copy-start | bytes 6148
  649.2 6.8 %copy-start.34 = (f32[2,256]{1,0:T(2,128)S(1)}, f32[2,256]{1,0:T(2,128)}, u32[]{:S(2)}) copy-start(f32[2,256]{1,0:T(2,128)} %copy-done.33) | copy-start | bytes 6148
  649.2 7.5 %copy-start.19 = (bf16[2,256,1024]{2,1,0:T(8,128)(2,1)S(1)}, bf16[2,256,1024]{2,1,0:T(8,128)(2,1)}, u32[]{:S(2)}) copy-start(bf16[2,256,1024]{2,1,0:T(8,128)(2,1)} %param.22) | copy-start | bytes 3145732
  649.2 7.5 %copy-start.41 = (pred[2,256]{1,0:T(4,128)(4,1)S(1)}, pred[2,256]{1,0:T(4,128)(4,1)}, u32[]{:S(2)}) copy-start(pred[2,256]{1,0:T(4,128)(4,1)} %copy-done.39) | copy-start | bytes 1540
  657.6 2.9 copy-start.10
  (10 other events, 12.3 us)
Sparse Core Ops, SparseCore 0:
  20.4 60.9 all-gather.2
  178.1 58.2 all-gather.4
  418.1 156.7 all-reduce.3
  577.5 71.6 reduce-scatter.1
where the time goes:
time: 674 us; the launch traced here: 669 us
  matrix products  241 us (36%)
  waiting for transfers between devices  208 us (31%)
  local copies, waits for them, and re-layouts  83.6 us (12%)
  other arithmetic  81.4 us (12%)
  blocking collectives  40.9 us (6%)
  between operations  14.7 us (2%)
    all_gather x2, waiting for transfers between devices, block_forward(): row_keyval = lax.all_gather(local_keyval, 'seq', axis=1, tiled=True)  92.2 us
    reduce_scatter x1, waiting for transfers between devices, per_device(): lax.psum_scatter(jnp.concatenate([grad_keys.reshape(tok_count * lax.axis_...  71.4 us
    psum x1, waiting for transfers between devices, per_device(): lax.psum((grad_table, grad_lift, grad_liftbias, grad_fan, grad_fanbias),...  43.9 us
    psum x1, blocking collectives, per_device(): lax.psum((grad_table, grad_lift, grad_liftbias, grad_fan, grad_fanbias),...  40.9 us
    dot_general x2, matrix products, block_forward(): jnp.einsum('rhqk,rkhd->rqhd', rounded, row_values, preferred_element_type...  34.7 us
    dot_general x2, matrix products, block_forward(): jnp.einsum('rqhd,rkhd->rhqk', queries, row_keys, preferred_element_type=j...  31.8 us
    reduce_sum x2, other arithmetic, block_forward(): jnp.sum(jnp.exp(scores - highest), axis=-1, keepdims=True)  29.7 us
    convert_element_type x1, other arithmetic, per_device(): grad_scores = (weights * (grad_weights - inner_sum)).astype(jnp.bfloat16)  28 us
  transfers between devices with their start and end apart: 4, of which 4 were waited for; matrix products, arithmetic and copies ran while one was open for 15% of the time, Pallas kernels for 0%

commit v1 on v0

v1 whole, which is shorter than its diff:
```python
import functools

import jax
import jax.numpy as jnp
from jax import lax
from jax.experimental import pallas as pl
from jax.experimental.pallas import tpu as pltpu
from jax.sharding import PartitionSpec as P

D = 1024
HEADS = 16
HEAD_DIM = 64
PAIRS = HEADS // 2
PREFIX = 10
PREFIX_PAD = 16
LEAST_LENGTH = 512
NN = (((1,), (0,)), ((), ()))
NT = (((1,), (1,)), ((), ()))
MIB = 1 << 20
BF16 = jnp.bfloat16
F32 = jnp.float32


def dot(left, right, dims=NN):
    return lax.dot_general(left, right, dims, preferred_element_type=F32)


def params(limit, steps):
    return pltpu.CompilerParams(
        dimension_semantics=("arbitrary",) * steps, vmem_limit_bytes=limit * MIB
    )


def normalize(values):
    centred = values - jnp.mean(values, axis=-1, keepdims=True)
    scale = lax.rsqrt(jnp.mean(centred * centred, axis=-1, keepdims=True) + 1e-05)
    return centred * scale, scale


def norm_back(grad, normed, scale):
    return scale * (
        grad
        - jnp.mean(grad, axis=-1, keepdims=True)
        - normed * jnp.mean(grad * normed, axis=-1, keepdims=True)
    )


def project_kernel(has_queries, tokens_ref, gain_ref, shift_ref, weight_ref, bias_ref, *rest):
    if has_queries:
        query_ref, keyval_ref, normed_ref = rest
    else:
        keyval_ref, normed_ref = rest
    step = pl.program_id(0)
    rows, toks = tokens_ref.shape[0], tokens_ref.shape[1]
    tile = weight_ref.shape[1]
    query_steps = D // tile if has_queries else 0

    @pl.when(step == 0)
    def _():
        normed, _ = normalize(tokens_ref[...].reshape(rows * toks, D).astype(F32))
        normed_ref[...] = (normed * gain_ref[...] + shift_ref[...]).astype(BF16)

    result = (dot(normed_ref[...], weight_ref[...]) + bias_ref[...]).astype(BF16)
    if has_queries:

        @pl.when(step < query_steps)
        def _():
            query_ref[...] = (result * 0.125).reshape(rows, toks, tile)

    @pl.when(step >= query_steps)
    def _():
        keyval_ref[...] = result.reshape(rows, 1, toks, tile)


def project(tokens, gain, shift, weight, bias, has_queries, tile=512):
    rows, toks, _ = tokens.shape
    tiles = D // tile
    query_steps = tiles if has_queries else 0
    first = 0 if has_queries else tiles
    out_shape = [jax.ShapeDtypeStruct((rows, 2, toks, D), BF16)]

    def keyval_map(step):
        at = jnp.maximum(step - query_steps, 0)
        return (0, at // tiles, 0, at % tiles)

    out_specs = [pl.BlockSpec((rows, 1, toks, tile), keyval_map)]
    if has_queries:
        out_shape.insert(0, jax.ShapeDtypeStruct((rows, toks, D), BF16))
        out_specs.insert(
            0, pl.BlockSpec((rows, toks, tile), lambda step: (0, 0, jnp.minimum(step, tiles - 1)))
        )
    steps = query_steps + 2 * tiles
    return pl.pallas_call(
        functools.partial(project_kernel, has_queries),
        grid=(steps,),
        in_specs=[
            pl.BlockSpec((rows, toks, D), lambda step: (0, 0, 0)),
            pl.BlockSpec((1, D), lambda step: (0, 0)),
            pl.BlockSpec((1, D), lambda step: (0, 0)),
            pl.BlockSpec((D, tile), lambda step: (0, step + first)),
            pl.BlockSpec((1, tile), lambda step: (0, step + first)),
        ],
        out_specs=out_specs,
        out_shape=out_shape,
        scratch_shapes=[pltpu.VMEM((rows * toks, D), BF16)],
        compiler_params=params(40, 1),
        cost_estimate=pl.CostEstimate(
            flops=2 * rows * toks * D * tile * steps,
            bytes_accessed=2 * (D * tile * steps + rows * toks * (D + tile * steps)),
            transcendentals=0,
        ),
        name="project_own" if has_queries else "project_up",
    )(tokens, gain, shift, weight, bias)


def head_lanes(values, head):
    lanes = lax.broadcasted_iota(jnp.int32, values.shape, 1)
    keep = lanes < HEAD_DIM if head == 0 else lanes >= HEAD_DIM
    return jnp.where(keep, values, jnp.zeros_like(values))


def prefix_mask(values, fill):
    places = lax.broadcasted_iota(jnp.int32, values.shape, 0)
    return jnp.where(places < PREFIX, values, fill)


class Places:
    def __init__(self, toks, level_count):
        self.toks = toks
        self.level_count = level_count

    def masked(self, block):
        if block < 2:
            return True
        level = block // 2
        return (self.level_count - level) * 2 * self.toks > LEAST_LENGTH

    def limits(self, place, length):
        base = place * self.toks
        queries = base + lax.broadcasted_iota(jnp.int32, (1, self.toks), 1)
        return jnp.minimum(queries, length - 1)

    def visible(self, block, place, limit):
        if block == 0:
            base = place * self.toks
        else:
            base = (lax.bitwise_xor(place, block % 2) - (block // 2) * 2) * self.toks
        keys = lax.broadcasted_iota(jnp.int32, (self.toks, self.toks), 0)
        return keys <= limit - base


def spread_prefix(prefix):
    tiled = jnp.concatenate([prefix] * HEADS, axis=0)
    rows = lax.broadcasted_iota(jnp.int32, tiled.shape, 0) // PREFIX_PAD
    cols = lax.broadcasted_iota(jnp.int32, tiled.shape, 1) // HEAD_DIM
    return jnp.where(rows == cols, tiled, jnp.zeros_like(tiled))


def attend_kernel(places, first_row, pair_step, place_ref, length_ref, query_all_ref, query_ref, *rest):
    block_count = 2 * places.level_count
    keyval_refs = rest[:block_count]
    prefix_all_ref, prefix_ref, mixed_ref, total_ref, spread_ref, scores_ref, hide_ref = rest[block_count:]
    place = place_ref[0]
    level = place // 2
    length = length_ref[first_row + pl.program_id(0)]
    limit = places.limits(place, length)
    step = pl.program_id(1)
    masked_blocks = [block for block in range(block_count) if places.masked(block)]

    @pl.when((pl.program_id(0) == 0) & (step == 0))
    def _():
        spread_ref[...] = spread_prefix(prefix_all_ref[0])

    @pl.when(step == 0)
    def _():
        scores_ref[...] = dot(spread_ref[...], query_all_ref[0], NT)
        for at, block in enumerate(masked_blocks):
            hide_ref[at] = jnp.where(places.visible(block, place, limit), 0.0, -jnp.inf)

    def attend(blocks):
        def scores_of(at):
            pair, head = at // 2, at % 2
            cols = slice(pair * 128, (pair + 1) * 128)
            queries = head_lanes(query_ref[0, :, cols], head)
            spread = scores_ref[pl.ds(pl.multiple_of((step * pair_step * 2 + at) * PREFIX_PAD, PREFIX_PAD), PREFIX_PAD), :]
            prefix_scores = prefix_mask(spread, -jnp.inf)
            highest = jnp.max(prefix_scores, axis=0, keepdims=True)
            scores = []
            for block in range(blocks):
                part = dot(keyval_refs[block][0, 0, :, cols], queries, NT)
                if places.masked(block):
                    part = part + hide_ref[masked_blocks.index(block)]
                highest = jnp.maximum(highest, jnp.max(part, axis=0, keepdims=True))
                scores.append(part)
            return prefix_scores, scores, highest

        ahead = scores_of(0)
        outs = []
        for at in range(2 * pair_step):
            pair, head = at // 2, at % 2
            cols = slice(pair * 128, (pair + 1) * 128)
            prefix_scores, scores, highest = ahead
            if at + 1 < 2 * pair_step:
                ahead = scores_of(at + 1)
            if head == 0:
                values_t = [keyval_refs[block][0, 1, :, cols].T for block in range(blocks)]
                prefix_values_t = prefix_ref[1, :, cols].T
            rows = slice(head * HEAD_DIM, (head + 1) * HEAD_DIM)
            prefix_weights = jnp.exp(prefix_scores - highest)
            total = jnp.sum(prefix_weights, axis=0, keepdims=True)
            mixed = dot(prefix_values_t[rows], prefix_weights.astype(BF16))
            for block in range(blocks):
                weights = jnp.exp(scores[block] - highest)
                total = total + jnp.sum(weights, axis=0, keepdims=True)
                mixed = mixed + dot(values_t[block][rows], weights.astype(BF16))
            outs.append(mixed * (1.0 / total))
            total_ref[0, at : at + 1, :] = highest + jnp.log(total)
            if head == 1:
                mixed_ref[0, :, cols] = jnp.concatenate(outs, axis=0).T.astype(BF16)
                outs = []

    for levels in range(places.level_count):

        @pl.when(level == levels)
        def _():
            attend(2 * (levels + 1))


def block_spec(shape, first_row, pair_last=True):
    if len(shape) == 3:
        return pl.BlockSpec(
            (1, shape[1], shape[2]), lambda row, pair, *_: (row + first_row, 0, pair)
        )
    return pl.BlockSpec(
        (1, shape[1], shape[2], shape[3]), lambda row, pair, *_: (row + first_row, 0, 0, pair)
    )


def attend(place, lengths, queries, keyvals, prefix_keyval, first_row, row_count, pair_step=4):
    toks = queries.shape[1]
    places = Places(toks, len(keyvals) // 2)
    width = 128 * pair_step
    return pl.pallas_call(
        functools.partial(attend_kernel, places, first_row, pair_step),
        grid_spec=pltpu.PrefetchScalarGridSpec(
            num_scalar_prefetch=2,
            grid=(row_count, PAIRS // pair_step),
            in_specs=[
                pl.BlockSpec((1, toks, D), lambda row, pair, *_: (row + first_row, 0, 0)),
                block_spec((1, toks, width), first_row),
            ]
            + [block_spec((1, 2, toks, width), row) for _, row in keyvals]
            + [
                pl.BlockSpec((2, PREFIX_PAD, D), lambda row, pair, *_: (0, 0, 0)),
                pl.BlockSpec((2, PREFIX_PAD, width), lambda row, pair, *_: (0, 0, pair)),
            ],
            out_specs=[
                block_spec((1, toks, width), 0),
                pl.BlockSpec((1, 2 * pair_step, toks), lambda row, pair, *_: (row, pair, 0)),
            ],
            scratch_shapes=[
                pltpu.VMEM((HEADS * PREFIX_PAD, D), BF16),
                pltpu.VMEM((HEADS * PREFIX_PAD, toks), F32),
                pltpu.VMEM((sum(places.masked(b) for b in range(len(keyvals))), toks, toks), F32),
            ],
        ),
        out_shape=[
            jax.ShapeDtypeStruct((row_count, toks, D), BF16),
            jax.ShapeDtypeStruct((row_count, HEADS, toks), F32),
        ],
        compiler_params=params(40, 2),
        cost_estimate=pl.CostEstimate(
            flops=row_count * 16 * 4 * toks * toks * len(keyvals) * 256,
            bytes_accessed=row_count * toks * D * 2 * (2 + 2 * len(keyvals)),
            transcendentals=row_count * HEADS * toks * toks * len(keyvals),
        ),
        name="attend",
    )(place, lengths, queries, queries, *[array for array, _ in keyvals], prefix_keyval, prefix_keyval)


def prefix_back_kernel(query_ref, grad_ref, mixed_ref, total_ref, prefix_ref, inner_ref, start_ref, prefix_grad_ref, spread_ref):
    row = pl.program_id(0)
    toks = query_ref.shape[1]

    @pl.when(row == 0)
    def _():
        spread_ref[0] = spread_prefix(prefix_ref[0])
        spread_ref[1] = spread_prefix(prefix_ref[1])
        prefix_grad_ref[...] = jnp.zeros_like(prefix_grad_ref)

    queries = query_ref[0]
    grads = grad_ref[0]
    product = grads.astype(F32) * mixed_ref[0].astype(F32)
    head_of = lax.broadcasted_iota(jnp.int32, (HEADS, D), 1) // HEAD_DIM
    chosen = jnp.where(head_of == lax.broadcasted_iota(jnp.int32, (HEADS, D), 0), 1.0, 0.0).astype(BF16)
    high = product.astype(BF16)
    low = (product - high.astype(F32)).astype(BF16)
    inner = dot(chosen, high, NT) + dot(chosen, low, NT)
    inner_ref[0] = inner

    def per_head(values):
        return values.reshape(HEADS, PREFIX_PAD, toks)

    scores = per_head(dot(spread_ref[0], queries, NT))
    grad_weights = per_head(dot(spread_ref[1], grads, NT))
    weights = jnp.exp(scores - total_ref[0][:, None, :])
    valid = lax.broadcasted_iota(jnp.int32, weights.shape, 1) < PREFIX
    weights = jnp.where(valid, weights, 0.0)
    grad_scores = weights * (grad_weights - inner[:, None, :])
    weights = weights.reshape(HEADS * PREFIX_PAD, toks).astype(BF16)
    grad_scores = grad_scores.reshape(HEADS * PREFIX_PAD, toks).astype(BF16)
    start_ref[0] = dot(grad_scores.T, spread_ref[0])
    own = (
        lax.broadcasted_iota(jnp.int32, (HEADS * PREFIX_PAD, D), 0) // PREFIX_PAD
        == lax.broadcasted_iota(jnp.int32, (HEADS * PREFIX_PAD, D), 1) // HEAD_DIM
    )

    def gather(values):
        return jnp.sum(jnp.where(own, values, 0.0).reshape(HEADS, PREFIX_PAD, D), axis=0)

    prefix_grad_ref[0] += gather(dot(grad_scores, queries))
    prefix_grad_ref[1] += gather(dot(weights, grads))


def prefix_back(queries, grads, mixed, total, prefix_keyval, first_row):
    row_count, toks, _ = grads.shape
    row_block = pl.BlockSpec((1, toks, D), lambda row: (row, 0, 0))
    head_block = pl.BlockSpec((1, HEADS, toks), lambda row: (row, 0, 0))
    return pl.pallas_call(
        prefix_back_kernel,
        grid=(row_count,),
        in_specs=[
            pl.BlockSpec((1, toks, D), lambda row: (row + first_row, 0, 0)),
            row_block,
            row_block,
            head_block,
            pl.BlockSpec((2, PREFIX_PAD, D), lambda row: (0, 0, 0)),
        ],
        out_specs=[
            head_block,
            row_block,
            pl.BlockSpec((2, PREFIX_PAD, D), lambda row: (0, 0, 0)),
        ],
        out_shape=[
            jax.ShapeDtypeStruct((row_count, HEADS, toks), F32),
            jax.ShapeDtypeStruct((row_count, toks, D), F32),
            jax.ShapeDtypeStruct((2, PREFIX_PAD, D), F32),
        ],
        scratch_shapes=[pltpu.VMEM((2, HEADS * PREFIX_PAD, D), BF16)],
        compiler_params=params(40, 1),
        cost_estimate=pl.CostEstimate(
            flops=row_count * 12 * toks * D * 256,
            bytes_accessed=row_count * toks * D * 10,
            transcendentals=row_count * toks * 256,
        ),
        name="prefix_back",
    )(queries, grads, mixed, total, prefix_keyval)


def attend_back_kernel(places, blocks, first_row, pair_step, final, place_ref, length_ref, query_ref, grad_ref, total_ref, inner_ref, start_ref, *rest):
    count = len(blocks)
    keyval_refs = dict(zip(blocks, rest[:count]))
    grad_query_ref = rest[count]
    out_refs = dict(zip(blocks, rest[count + 1 : 2 * count + 1]))
    hide_ref = rest[2 * count + 1]
    place = place_ref[0]
    level = place // 2
    length = length_ref[first_row + pl.program_id(0)]
    limit = places.limits(place, length)
    masked_blocks = [block for block in blocks if places.masked(block)]

    if masked_blocks:

        @pl.when(pl.program_id(1) == 0)
        def _():
            for at, block in enumerate(masked_blocks):
                hide_ref[at] = jnp.where(places.visible(block, place, limit), 0.0, -jnp.inf)

    def back(active):
        def products_of(at):
            pair, head = at // 2, at % 2
            cols = slice(pair * 128, (pair + 1) * 128)
            queries = head_lanes(query_ref[0, :, cols], head)
            grads = head_lanes(grad_ref[0, :, cols], head)
            scores = {}
            grad_weights = {}
            for block in active:
                part = dot(keyval_refs[block][0, 0, :, cols], queries, NT)
                if block in masked_blocks:
                    part = part + hide_ref[masked_blocks.index(block)]
                scores[block] = part
                grad_weights[block] = dot(keyval_refs[block][0, 1, :, cols], grads, NT)
            return queries, grads, scores, grad_weights

        ahead = products_of(0)
        for at in range(2 * pair_step):
            pair, head = at // 2, at % 2
            cols = slice(pair * 128, (pair + 1) * 128)
            queries, grads, scores, grad_weights = ahead
            if at + 1 < 2 * pair_step:
                ahead = products_of(at + 1)
            if head == 0:
                keys_t = {block: keyval_refs[block][0, 0, :, cols].T for block in active}
                grad_keys = {}
                grad_values = {}
                outs = []
            total = total_ref[0, at : at + 1, :]
            inner = inner_ref[0, at : at + 1, :]
            rows = slice(head * HEAD_DIM, (head + 1) * HEAD_DIM)
            grad_query = None
            for block in active:
                weights = jnp.exp(scores[block] - total)
                grad_scores = (weights * (grad_weights[block] - inner)).astype(BF16)
                part_values = dot(weights.astype(BF16), grads)
                part_keys = dot(grad_scores, queries)
                part_query = dot(keys_t[block][rows], grad_scores)
                if head == 0:
                    grad_values[block], grad_keys[block] = part_values, part_keys
                else:
                    out_refs[block][0, 0, :, cols] = (grad_keys[block] + part_keys).astype(BF16)
                    out_refs[block][0, 1, :, cols] = (grad_values[block] + part_values).astype(BF16)
                grad_query = part_query if grad_query is None else grad_query + part_query
            outs.append(grad_query)
            if head == 1:
                grad_query = jnp.concatenate(outs, axis=0).T + start_ref[0, :, cols]
                if final:
                    grad_query = (grad_query * 0.125).astype(BF16)
                grad_query_ref[0, :, cols] = grad_query

    for levels in range(places.level_count):
        active = [block for block in blocks if block < 2 * (levels + 1)]

        @pl.when(level == levels)
        def _():
            if active:
                back(active)
            else:
                grad_query_ref[...] = start_ref[...]


def attend_back(place, lengths, queries, grads, total, inner, start, keyvals, level_count, first_row, final, pair_step=4):
    row_count, toks, _ = grads.shape
    blocks = sorted(keyvals)
    places = Places(toks, level_count)
    width = 128 * pair_step
    row_block = block_spec((1, toks, width), 0)
    head_block = pl.BlockSpec((1, 2 * pair_step, toks), lambda row, pair, *_: (row, pair, 0))
    masked = max(1, sum(places.masked(block) for block in blocks))
    return pl.pallas_call(
        functools.partial(attend_back_kernel, places, blocks, first_row, pair_step, final),
        grid_spec=pltpu.PrefetchScalarGridSpec(
            num_scalar_prefetch=2,
            grid=(row_count, PAIRS // pair_step),
            in_specs=[block_spec((1, toks, width), first_row), row_block, head_block, head_block, row_block]
            + [block_spec((1, 2, toks, width), keyvals[block][1]) for block in blocks],
            out_specs=[row_block] + [block_spec((1, 2, toks, width), 0)] * len(blocks),
            scratch_shapes=[pltpu.VMEM((masked, toks, toks), F32)],
        ),
        out_shape=[jax.ShapeDtypeStruct((row_count, toks, D), BF16 if final else F32)]
        + [jax.ShapeDtypeStruct((row_count, 2, toks, D), BF16)] * len(blocks),
        compiler_params=params(48, 2),
        cost_estimate=pl.CostEstimate(
            flops=row_count * HEADS * 10 * toks * toks * len(blocks) * 256,
            bytes_accessed=row_count * toks * D * 2 * (5 + 4 * len(blocks)),
            transcendentals=row_count * HEADS * toks * toks * len(blocks),
        ),
        name="attend_back",
    )(place, lengths, queries, grads, total, inner, start, *[keyvals[block][0] for block in blocks])


GELU_SCALE = 0.7978845608028654
GELU_CUBE = 0.044715


def feed_forward_kernel(first_row, sub, place_ref, length_ref, source_ref, tokens_ref, cotangent_ref, mixed_ref, output_weight_ref, output_bias_ref, gain_ref, shift_ref, expand_weight_ref, expand_bias_ref, contract_weight_ref, contract_bias_ref, *rest):
    activations_ref, grad_residual_ref, grad_heads_ref, residual_ref, normed_ref, grad_out_ref, active_ref, grad_expand_ref, result_ref, grad_normed_ref = rest[-10:]
    step = pl.program_id(0)
    rows, toks, _ = tokens_ref.shape
    count = rows * toks
    tile = expand_weight_ref.shape[1]

    @pl.when(step == 0)
    def _():
        projected = dot(mixed_ref[...].reshape(count, D), output_weight_ref[...])
        residual = tokens_ref[...].reshape(count, D).astype(F32) + projected + output_bias_ref[...]
        residual_ref[...] = residual
        normed, _ = normalize(residual)
        normed_ref[...] = (normed * gain_ref[...] + shift_ref[...]).astype(BF16)
        spots = place_ref[0] * toks + lax.broadcasted_iota(jnp.int32, (toks, D), 0)
        for row in range(rows):
            target = (spots >= source_ref[first_row + row]) & (spots < length_ref[first_row + row])
            values = cotangent_ref[row].astype(F32)
            grad_out_ref[row * toks : (row + 1) * toks, :] = jnp.where(target, values, 0.0).astype(BF16)

    for at in range(tile // sub):
        cols = slice(at * sub, (at + 1) * sub)
        values = dot(normed_ref[...], expand_weight_ref[:, cols]) + expand_bias_ref[:, cols]
        grad_hidden = dot(grad_out_ref[...], contract_weight_ref[cols, :], NT)
        square = values * values
        bend = jnp.tanh(values * (GELU_SCALE + GELU_SCALE * GELU_CUBE * square))
        half = 0.5 * (1.0 + bend)
        slope = half + (0.5 * values) * (1.0 - bend * bend) * (
            GELU_SCALE + 3.0 * GELU_SCALE * GELU_CUBE * square
        )
        active_ref[:, cols] = (values * half).astype(BF16)
        grad_expand_ref[:, cols] = (grad_hidden * slope).astype(BF16)

    part = dot(active_ref[...], contract_weight_ref[...])
    grad_part = dot(grad_expand_ref[...], expand_weight_ref[...], NT)

    @pl.when(step == 0)
    def _():
        result_ref[...] = part
        grad_normed_ref[...] = grad_part

    @pl.when(step > 0)
    def _():
        result_ref[...] += part
        grad_normed_ref[...] += grad_part

    @pl.when(step == pl.num_programs(0) - 1)
    def _():
        residual = residual_ref[...]
        activations_ref[...] = (residual + result_ref[...] + contract_bias_ref[...]).astype(BF16).reshape(rows, toks, D)
        normed, scale = normalize(residual)
        grad = grad_out_ref[...].astype(F32) + norm_back(grad_normed_ref[...] * gain_ref[...], normed, scale)
        grad_residual_ref[...] = grad.reshape(rows, toks, D)
        heads = dot(grad.astype(BF16), output_weight_ref[...], NT)
        grad_heads_ref[...] = heads.astype(BF16).reshape(rows, toks, D)


def feed_forward(place, lengths, sources, tokens, cotangent, mixed, weights, first_row, earlier, tile=512, sub=256):
    row_count, toks, _ = mixed.shape
    count = row_count * toks
    output_weight, output_bias, gain, shift, expand_weight, expand_bias, contract_weight, contract_bias = weights
    hidden = expand_weight.shape[1]
    given = [] if earlier is None else [earlier]
    at_row = first_row // row_count

    def whole(shape):
        return pl.BlockSpec(shape, lambda step, *_: (0,) * len(shape))

    some_rows = pl.BlockSpec((row_count, toks, D), lambda step, *_: (at_row, 0, 0))
    return pl.pallas_call(
        functools.partial(feed_forward_kernel, first_row, sub),
        grid_spec=pltpu.PrefetchScalarGridSpec(
            num_scalar_prefetch=3,
            grid=(hidden // tile,),
            in_specs=[
                some_rows,
                some_rows,
                whole((row_count, toks, D)),
                whole((D, D)),
                whole((1, D)),
                whole((1, D)),
                whole((1, D)),
                pl.BlockSpec((D, tile), lambda step, *_: (0, step)),
                pl.BlockSpec((1, tile), lambda step, *_: (0, step)),
                pl.BlockSpec((tile, D), lambda step, *_: (step, 0)),
                whole((1, D)),
            ]
            + [pl.BlockSpec(memory_space=pl.ANY)] * len(given),
            out_specs=[some_rows, whole((row_count, toks, D)), whole((row_count, toks, D))],
            scratch_shapes=[
                pltpu.VMEM((count, D), F32),
                pltpu.VMEM((count, D), BF16),
                pltpu.VMEM((count, D), BF16),
                pltpu.VMEM((count, tile), BF16),
                pltpu.VMEM((count, tile), BF16),
                pltpu.VMEM((count, D), F32),
                pltpu.VMEM((count, D), F32),
            ],
        ),
        out_shape=[
            jax.ShapeDtypeStruct(tokens.shape, BF16),
            jax.ShapeDtypeStruct((row_count, toks, D), F32),
            jax.ShapeDtypeStruct((row_count, toks, D), BF16),
        ],
        input_output_aliases={14: 0} if given else {},
        compiler_params=params(56, 1),
        cost_estimate=pl.CostEstimate(
            flops=count * D * (8 * hidden + 4 * D),
            bytes_accessed=4 * D * hidden + 2 * D * D + 16 * count * D,
            transcendentals=count * hidden,
        ),
        name="feed_forward",
    )(place, lengths, sources, tokens, cotangent, mixed, output_weight, output_bias, gain, shift, expand_weight, expand_bias, contract_weight, contract_bias, *given)


def up_back_kernel(own_ref, received_ref, weight_ref, grad_ref, total_ref):
    step = pl.program_id(0)
    rows, _, toks, tile = own_ref.shape
    values = (own_ref[...].astype(F32) + received_ref[...].astype(F32)).astype(BF16)
    part = dot(values.reshape(rows * toks, tile), weight_ref[...], NT)

    @pl.when(step == 0)
    def _():
        total_ref[...] = part

    @pl.when(step > 0)
    def _():
        total_ref[...] += part

    @pl.when(step == pl.num_programs(0) - 1)
    def _():
        grad_ref[...] = total_ref[...].astype(BF16).reshape(rows, toks, D)


def up_back(own, received, weight, tile=512):
    rows, _, toks, _ = own.shape
    tiles = D // tile
    keyval = pl.BlockSpec((rows, 1, toks, tile), lambda step: (0, step // tiles, 0, step % tiles))
    return pl.pallas_call(
        up_back_kernel,
        grid=(2 * tiles,),
        in_specs=[keyval, keyval, pl.BlockSpec((D, tile), lambda step: (0, step + tiles))],
        out_specs=pl.BlockSpec((rows, toks, D), lambda step: (0, 0, 0)),
        out_shape=jax.ShapeDtypeStruct((rows, toks, D), BF16),
        scratch_shapes=[pltpu.VMEM((rows * toks, D), F32)],
        compiler_params=params(40, 1),
        cost_estimate=pl.CostEstimate(
            flops=4 * rows * toks * D * D, bytes_accessed=4 * D * D + 10 * rows * toks * D, transcendentals=0
        ),
        name="up_back",
    )(own, received, weight)


def project_back_kernel(level_count, tokens_ref, gain_ref, residual_ref, query_ref, own_ref, received_ref, weight_ref, *rest):
    above_refs = rest[: level_count - 1]
    grad_ref, total_ref = rest[-2:]
    step = pl.program_id(0)
    rows, toks, tile = query_ref.shape
    count = rows * toks
    query_steps = D // tile

    @pl.when(step == 0)
    def _():
        total_ref[...] = dot(query_ref[...].reshape(count, tile), weight_ref[...], NT)

    @pl.when((step > 0) & (step < query_steps))
    def _():
        total_ref[...] += dot(query_ref[...].reshape(count, tile), weight_ref[...], NT)

    @pl.when(step >= query_steps)
    def _():
        values = (own_ref[...].astype(F32) + received_ref[...].astype(F32)).astype(BF16)
        total_ref[...] += dot(values.reshape(count, tile), weight_ref[...], NT)

    @pl.when(step == pl.num_programs(0) - 1)
    def _():
        total = total_ref[...]
        for above_ref in above_refs:
            total = total + above_ref[...].reshape(count, D).astype(F32)
        normed, scale = normalize(tokens_ref[...].reshape(count, D).astype(F32))
        grad = norm_back(total * gain_ref[...], normed, scale)
        grad_ref[...] = residual_ref[...] + grad.reshape(rows, toks, D)


def project_back(tokens, gain, grad_residual, grad_queries, own, received, weight, above, first_row, earlier, tile=512):
    row_count, toks, _ = grad_queries.shape
    count = row_count * toks
    tiles = D // tile
    at_row = first_row // row_count
    given = [] if earlier is None else [earlier]

    def keyval_map(step):
        at = jnp.maximum(step - tiles, 0)
        return (0, at // tiles, 0, at % tiles)

    some_rows = pl.BlockSpec((row_count, toks, D), lambda step: (at_row, 0, 0))
    all_rows = pl.BlockSpec((row_count, toks, D), lambda step: (0, 0, 0))
    keyval = pl.BlockSpec((row_count, 1, toks, tile), keyval_map)
    return pl.pallas_call(
        functools.partial(project_back_kernel, len(above) + 1),
        grid=(3 * tiles,),
        in_specs=[
            some_rows,
            pl.BlockSpec((1, D), lambda step: (0, 0)),
            all_rows,
            pl.BlockSpec((row_count, toks, tile), lambda step: (0, 0, jnp.minimum(step, tiles - 1))),
            keyval,
            keyval,
            pl.BlockSpec((D, tile), lambda step: (0, step)),
        ]
        + [all_rows] * len(above)
        + [pl.BlockSpec(memory_space=pl.ANY)] * len(given),
        out_specs=some_rows,
        out_shape=jax.ShapeDtypeStruct(tokens.shape, F32),
        scratch_shapes=[pltpu.VMEM((count, D), F32)],
        input_output_aliases={7 + len(above): 0} if given else {},
        compiler_params=params(40, 1),
        cost_estimate=pl.CostEstimate(
            flops=6 * count * D * D, bytes_accessed=6 * D * D + 20 * count * D, transcendentals=0
        ),
        name="project_back",
    )(tokens, gain, grad_residual, grad_queries, own, received, weight, *above, *given)


def prefix_kernel(table_ref, lift_ref, lift_bias_ref, fan_ref, fan_bias_ref, lifted_ref, keyval_ref):
    lifted = jnp.tanh(dot(table_ref[...], lift_ref[...]) + lift_bias_ref[...])
    lifted_ref[...] = jnp.zeros_like(lifted_ref)
    lifted_ref[:PREFIX, :] = lifted
    keyval_ref[...] = jnp.zeros_like(keyval_ref)
    keyval = (dot(lifted.astype(BF16), fan_ref[...]) + fan_bias_ref[...]).astype(BF16)
    keyval_ref[0, :PREFIX, :] = keyval[:, :D]
    keyval_ref[1, :PREFIX, :] = keyval[:, D:]


def prefix_forward(table, lift, lift_bias, fan, fan_bias):
    return pl.pallas_call(
        prefix_kernel,
        out_shape=[
            jax.ShapeDtypeStruct((PREFIX_PAD, lift.shape[1]), F32),
            jax.ShapeDtypeStruct((2, PREFIX_PAD, D), BF16),
        ],
        compiler_params=pltpu.CompilerParams(vmem_limit_bytes=32 * MIB),
        name="prefix_forward",
    )(table, lift, lift_bias, fan, fan_bias)


def dot_split(left, right, dims=NN):
    if left.dtype == F32:
        high = left.astype(BF16)
        return dot(high, right, dims) + dot((left - high.astype(F32)).astype(BF16), right, dims)
    high = right.astype(BF16)
    return dot(left, high, dims) + dot(left, (right - high.astype(F32)).astype(BF16), dims)


def prefix_network_back_kernel(grad_ref, table_ref, lift_ref, fan_ref, lifted_ref, grad_table_ref, grad_lift_ref, grad_lift_bias_ref, grad_fan_ref, grad_fan_bias_ref):
    lifted = lifted_ref[...]
    lifted_t = lifted.astype(BF16).T
    grad_lifted = None
    for half in range(2):
        cols = slice(half * D, (half + 1) * D)
        grad = grad_ref[half]
        grad_fan_bias_ref[:, cols] = jnp.sum(grad, axis=0, keepdims=True)
        grad_fan_ref[:, cols] = dot_split(lifted_t, grad)
        part = dot_split(grad, fan_ref[:, cols], NT)
        grad_lifted = part if grad_lifted is None else grad_lifted + part
    grad_lifted = grad_lifted * (1.0 - lifted * lifted)
    grad_lift_bias_ref[...] = jnp.sum(grad_lifted, axis=0, keepdims=True)
    table = jnp.concatenate([table_ref[...], jnp.zeros((PREFIX_PAD - PREFIX, D), F32)], axis=0)
    grad_lift_ref[...] = dot_split(table.T.astype(BF16), grad_lifted)
    grad_table_ref[...] = dot_split(grad_lifted, lift_ref[...], NT)[:PREFIX]


def prefix_network_back(grad, table, lift, fan, lifted):
    hidden = lift.shape[1]
    return pl.pallas_call(
        prefix_network_back_kernel,
        out_shape=[
            jax.ShapeDtypeStruct((PREFIX, D), F32),
            jax.ShapeDtypeStruct((D, hidden), F32),
            jax.ShapeDtypeStruct((1, hidden), F32),
            jax.ShapeDtypeStruct((hidden, 2 * D), F32),
            jax.ShapeDtypeStruct((1, 2 * D), F32),
        ],
        compiler_params=pltpu.CompilerParams(vmem_limit_bytes=40 * MIB),
        name="prefix_network_back",
    )(grad, table.astype(F32), lift, fan, lifted)


def sum_everywhere(values, axes):
    for axis in axes:
        size = lax.axis_size(axis)
        if size & (size - 1):
            values = lax.psum(values, axis)
            continue
        hop = 1
        while hop < size:
            values = values + lax.ppermute(values, axis, [(at, at ^ hop) for at in range(size)])
            hop *= 2
    return values


def per_device(tokens, cotangent, row_lengths, source_lengths, first_gain, first_shift, attend_weight, attend_bias, output_weight, output_bias, second_gain, second_shift, expand_weight, expand_bias, contract_weight, contract_bias, prefix_table, lift_weight, lift_bias, fan_weight, fan_bias):
    rows = tokens.shape[0]
    seq = lax.axis_size("seq")
    level_count = seq // 2
    levels = range(1, level_count)
    mates = [(at, at ^ 1) for at in range(seq)]
    place = lax.axis_index("seq").astype(jnp.int32).reshape(1)
    first_gain, first_shift, attend_bias, output_bias, second_gain, second_shift, expand_bias, contract_bias, lift_bias, fan_bias = [
        vector.reshape(1, -1)
        for vector in (first_gain, first_shift, attend_bias, output_bias, second_gain, second_shift, expand_bias, contract_bias, lift_bias, fan_bias)
    ]
    weights = (output_weight, output_bias, second_gain, second_shift, expand_weight, expand_bias, contract_weight, contract_bias)
    lower_tokens = [
        [lax.ppermute(tokens[row : row + 1], "seq", [(at, at + 2 * level) for at in range(seq - 2 * level)]) for level in levels]
        for row in range(rows)
    ]
    queries, keyval = project(tokens, first_gain, first_shift, attend_weight, attend_bias, True)
    mate_keyval = lax.ppermute(keyval, "seq", mates)
    lifted, prefix_keyval = prefix_forward(prefix_table, lift_weight, lift_bias, fan_weight, fan_bias)

    activations = None
    input_grad = None
    prefix_grad = None
    for row in range(rows):
        keyvals = [(keyval, row), (mate_keyval, row)]
        for level in levels:
            (lower,) = project(lower_tokens[row][level - 1], first_gain, first_shift, attend_weight, attend_bias, False)
            keyvals += [(lower, 0), (lax.ppermute(lower, "seq", mates), 0)]
        mixed, total = attend(place, row_lengths, queries, keyvals, prefix_keyval, row, 1)
        activations, grad_residual, grad_heads = feed_forward(
            place, row_lengths, source_lengths, tokens, cotangent, mixed, weights, row, activations
        )
        inner, start, row_prefix_grad = prefix_back(queries, grad_heads, mixed, total, prefix_keyval, row)
        prefix_grad = row_prefix_grad if prefix_grad is None else prefix_grad + row_prefix_grad
        grad_queries, *grads = attend_back(
            place, row_lengths, queries, grad_heads, total, inner, start, dict(enumerate(keyvals)), level_count, row, True
        )
        received = lax.ppermute(grads[1], "seq", mates)
        above = []
        for level in levels:
            from_mate = lax.ppermute(grads[2 * level + 1], "seq", mates)
            part = up_back(grads[2 * level], from_mate, attend_weight)
            above.append(lax.ppermute(part, "seq", [(at + 2 * level, at) for at in range(seq - 2 * level)]))
        input_grad = project_back(tokens, first_gain, grad_residual, grad_queries, grads[0], received, attend_weight, above, row, input_grad)
    prefix_grad = sum_everywhere(prefix_grad, ("seq", "dp"))
    grad_table, grad_lift, grad_lift_bias, grad_fan, grad_fan_bias = prefix_network_back(prefix_grad, prefix_table, lift_weight, fan_weight, lifted)
    return (activations, input_grad, grad_table, grad_lift, grad_lift_bias.reshape(-1), grad_fan, grad_fan_bias.reshape(-1))


def solution(mesh):
    batch = P("dp", "seq", None)
    return jax.shard_map(
        per_device,
        mesh=mesh,
        in_specs=(batch, batch, P("dp"), P("dp")) + (P(),) * 17,
        out_specs=(batch, batch, P(), P(), P(), P(), P()),
        check_vma=False,
    )
```

time: 674 us -> 208 us (0.31)
  matrix products: 241 us -> 0 us
  waiting for transfers between devices: 208 us -> 32.6 us
  Pallas kernels: 0 us -> 114 us
  other arithmetic: 81.4 us -> 0.1 us
  local copies, waits for them, and re-layouts: 83.6 us -> 19.9 us
  blocking collectives: 40.9 us -> 0 us
  starting transfers between devices: 0.34 us -> 37.6 us
  between operations: 14.7 us -> 1.35 us
    dot_general x32 -> x0, matrix products: 241 us -> none  [the longest x2 34.7 us: block_forward(): jnp.einsum('rhqk,rkhd->rqhd', rounded, row_values, preferred_element_type...]
    pallas_call x0 -> x17, Pallas kernels: none -> 114 us  [the longest x2 41.9 us: feed_forward(): pl.pallas_call(functools.partial(feed_forward_kernel, first_row, sub), gr...]
    all_gather x2 -> x0, waiting for transfers between devices: 92.2 us -> none  [block_forward(): row_keyval = lax.all_gather(local_keyval, 'seq', axis=1, tiled=True)]
    reduce_scatter x1 -> x0, waiting for transfers between devices: 71.4 us -> none  [per_device(): lax.psum_scatter(jnp.concatenate([grad_keys.reshape(tok_count * lax.axis_...]
    slice x13 -> x1, local copies, waits for them, and re-layouts: 48.3 us -> 0.86 us  [per_device(): tokens[row:row + 1]]
    psum x1 -> x0, waiting for transfers between devices: 43.9 us -> none  [per_device(): lax.psum((grad_table, grad_lift, grad_liftbias, grad_fan, grad_fanbias),...]
    psum x1 -> x0, blocking collectives: 40.9 us -> none  [per_device(): lax.psum((grad_table, grad_lift, grad_liftbias, grad_fan, grad_fanbias),...]
    reduce_sum x14 -> x0, other arithmetic: 38.4 us -> none  [the longest x2 29.7 us: block_forward(): jnp.sum(jnp.exp(scores - highest), axis=-1, keepdims=True)]
  transfers between devices with their start and end apart: 4 -> 16, of which waited for: 4 -> 5; matrix products, arithmetic and copies ran while one was open for 15% -> 0% of each run, Pallas kernels for 0% -> 49%
where the time goes in v1:
time: 208 us; the launch traced here: 205 us
  Pallas kernels  114 us (55%)
  starting transfers between devices  37.6 us (18%)
  waiting for transfers between devices  32.6 us (16%)
  local copies, waits for them, and re-layouts  19.9 us (10%)
    pallas_call x2, Pallas kernels, feed_forward(): pl.pallas_call(functools.partial(feed_forward_kernel, first_row, sub), gr...  41.9 us
    ppermute x5, starting transfers between devices, sum_everywhere(): lax.ppermute(values, axis, [(at, at ^ hop) for at in range(size)])  22.9 us
    ppermute x2, waiting for transfers between devices, per_device(): lax.ppermute(tokens[row:row + 1], 'seq', [(at, at + 2 * level) for at in...  22.1 us
    unnamed x94, local copies, waits for them, and re-layouts  19 us
    pallas_call x2, Pallas kernels, attend_back(): pl.pallas_call(functools.partial(attend_back_kernel, places, blocks, firs...  18.5 us
    pallas_call x3, Pallas kernels, project(): pl.pallas_call(functools.partial(project_kernel, has_queries), grid=(step...  14.1 us
    pallas_call x2, Pallas kernels, attend(): pl.pallas_call(functools.partial(attend_kernel, places, first_row, pair_s...  13.8 us
    pallas_call x2, Pallas kernels, project_back(): pl.pallas_call(functools.partial(project_back_kernel, len(above) + 1), gr...  11 us
  transfers between devices with their start and end apart: 16, of which 5 were waited for; matrix products, arithmetic and copies ran while one was open for 0% of the time, Pallas kernels for 49%

profile of v1, /device:TPU:0, one launch (start us, length us, event | category | flops | bytes accessed | tf_op | source)
XLA Modules:
  0.0 205.2 jit_solution(500286469376549697)
XLA Ops:
  0.6 2.8 %copy-done = bf16[1024,3072]{1,0:T(8,128)(2,1)S(1)} copy-done((bf16[1024,3072]{1,0:T(8,128)(2,1)S(1)}, bf16[1024,3072]{1,0:T(8,128)(2,1)}, u32[]{:S(2)}) %copy-start) | copy-done | bytes 6291480
  3.4 1.2 copy-done.3
  4.6 0.7 copy-done.17
  5.3 0.7 copy-done.19
  6.0 0.7 copy-done.21
  6.7 6.9 %project_own.1 = (bf16[2,256,1024]{2,1,0:T(8,128)(2,1)S(1)}, bf16[2,2,256,1024]{3,2,1,0:T(8,128)(2,1)}) custom-call(bf16[2,256,1024]{2,1,0:T(8,128)(2,1)S(1)} %copy-done.3, f32[1,1024]{1,0:T(1,128)S(1)} %bitcast.15, f32[1,1024]{1,0:T(1,128)S(1)} %bitcast.23, bf16[1024,3072]{1,0:T(8,128)(2,1)S(1)} %copy-done, f32[1,3072]{1,0:T(1,128)S(1)} %bitcast.20), custom_call_target="tpu_custom_call" | custom-call | flops 3221225472 | bytes 10485760 | tf_op jit(solution)/shard_map/project_own/pallas_call | solution.py:93
  14.1 0.9 fusion
  15.0 4.8 %collective-permute-start.3 = (bf16[1,256,1024]{2,1,0:T(8,128)(2,1)S(1)}, bf16[1,256,1024]{2,1,0:T(8,128)(2,1)S(1)}, u32[]{:S(2)}, u32[]{:S(2)}) collective-permute-start(bf16[1,256,1024]{2,1,0:T(8,128)(2,1)S(1)} %get-tuple-element.77), channel_id=1, source_target_pairs={{0,16},{8,24},{1,17},{9,25},{2,18},{10,26},{3,19},{11,27},{4,20},{... | collective-permute-start | bytes 1572872 | tf_op jit(solution)/shard_map/ppermute | solution.py:789
  19.7 11.7 %collective-permute-done.3.tokens_ref = bf16[1,256,1024]{2,1,0:T(8,128)(2,1)S(1)} collective-permute-done((bf16[1,256,1024]{2,1,0:T(8,128)(2,1)S(1)}, bf16[1,256,1024]{2,1,0:T(8,128)(2,1)S(1)}, u32[]{:S(2)}, u32[]{:S(2)}) %collective-permute-start.3) | collective-permute-done | bytes 524320 | tf_op jit(solution)/shard_map/ppermute | solution.py:789
  31.5 3.4 %project_up.3.rest_2_ = bf16[1,2,256,1024]{3,2,1,0:T(8,128)(2,1)} custom-call(bf16[1,256,1024]{2,1,0:T(8,128)(2,1)S(1)} %collective-permute-done.3.tokens_ref, f32[1,1024]{1,0:T(1,128)S(1)} %bitcast.16, f32[1,1024]{1,0:T(1,128)S(1)} %bitcast.24, bf16[1024,3072]{1,0:T(8,128)(2,1)S(1)} %copy-done.1, f32[1,3072]{1,0:T(1,128)S(1)} %bitcast.21), custom_call_target="tpu_custom_call" | custom-call | flops 1073741824 | bytes 5767168 | tf_op jit(solution)/shard_map/project_up/pallas_call | solution.py:93
  34.9 5.5 %collective-permute-start.1 = (bf16[1,256,1024]{2,1,0:T(8,128)(2,1)}, bf16[1,256,1024]{2,1,0:T(8,128)(2,1)}, u32[]{:S(2)}, u32[]{:S(2)}) collective-permute-start(bf16[1,256,1024]{2,1,0:T(8,128)(2,1)} %get-tuple-element.78), channel_id=1, source_target_pairs={{0,16},{8,24},{1,17},{9,25},{2,18},{10,26},{3,19},{11,27},{4,20},{... | collective-permute-start | bytes 1572872 | tf_op jit(solution)/shard_map/ppermute | solution.py:789
  40.6 0.6 prefix_forward.1
  41.2 10.3 %collective-permute-done.1.tokens_ref = bf16[1,256,1024]{2,1,0:T(8,128)(2,1)} collective-permute-done((bf16[1,256,1024]{2,1,0:T(8,128)(2,1)}, bf16[1,256,1024]{2,1,0:T(8,128)(2,1)}, u32[]{:S(2)}, u32[]{:S(2)}) %collective-permute-start.1) | collective-permute-done | bytes 524320 | tf_op jit(solution)/shard_map/ppermute | solution.py:789
  51.5 2.8 %copy-done.2 = bf16[1024,3072]{1,0:T(8,128)(2,1)S(1)} copy-done((bf16[1024,3072]{1,0:T(8,128)(2,1)S(1)}, bf16[1024,3072]{1,0:T(8,128)(2,1)}, u32[]{:S(2)}) %copy-start.2) | copy-done | bytes 6291480
  54.3 3.8 %project_up.2.rest_2_ = bf16[1,2,256,1024]{3,2,1,0:T(8,128)(2,1)S(1)} custom-call(bf16[1,256,1024]{2,1,0:T(8,128)(2,1)} %collective-permute-done.1.tokens_ref, f32[1,1024]{1,0:T(1,128)S(1)} %bitcast.17, f32[1,1024]{1,0:T(1,128)S(1)} %bitcast.25, bf16[1024,3072]{1,0:T(8,128)(2,1)S(1)} %copy-done.2, f32[1,3072]{1,0:T(1,128)S(1)} %bitcast.22), custom_call_target="tpu_custom_call" | custom-call | flops 1073741824 | bytes 5767168 | tf_op jit(solution)/shard_map/project_up/pallas_call | solution.py:93
  58.2 6.8 %attend.3 = (bf16[1,256,1024]{2,1,0:T(8,128)(2,1)S(1)}, f32[1,16,256]{2,1,0:T(8,128)S(1)}) custom-call(s32[1]{0:T(128)} %bitcast.place_ref, s32[2]{0:T(128)S(1)} %copy-done.28, bf16[2,256,1024]{2,1,0:T(8,128)(2,1)S(1)} %copy-done.32, bf16[2,256,1024]{2,1,0:T(8,128)(2,1)S(1)} %copy-done.32, bf16[2,2,256,1024]{3,2,1,0:T(8,128)(2,1)} %get-tuple-element.43.rest_0_, ...), custom_call_target="tpu_custom_call" | custom-call | flops 4294967296 | bytes 5242880 | tf_op jit(solution)/shard_map/attend/pallas_call | solution.py:243
  65.0 0.8 copy-done.43
  65.8 20.9 %feed_forward.2 = (bf16[2,256,1024]{2,1,0:T(8,128)(2,1)}, f32[1,256,1024]{2,1,0:T(8,128)}, bf16[1,256,1024]{2,1,0:T(8,128)(2,1)}) custom-call(s32[1]{0:T(128)} %bitcast.place_ref, s32[2]{0:T(128)} %length_ref.11, s32[2]{0:T(128)} %source_ref.3, bf16[2,256,1024]{2,1,0:T(8,128)(2,1)} %tokens_ref.9, bf16[2,256,1024]{2,1,0:T(8,128)(2,1)} %cotangent_ref.3, ...), custom_call_target="tpu_custom_call" | custom-call | flops 9663676416 | bytes 23068672 | tf_op jit(solution)/shard_map/feed_forward/pallas_call | solution.py:544
  86.7 1.0 copy-done.39
  87.8 1.3 prefix_back.3
  89.1 1.0 copy-done.36
  90.1 9.3 %attend_back.3 = (bf16[1,256,1024]{2,1,0:T(8,128)(2,1)S(1)}, bf16[1,2,256,1024]{3,2,1,0:T(8,128)(2,1)S(1)}, bf16[1,2,256,1024]{3,2,1,0:T(8,128)(2,1)S(1)}, bf16[...) custom-call(s32[1]{0:T(128)} %bitcast.place_ref, s32[2]{0:T(128)S(1)} %copy-done.29, ...), custom_call_target="tpu_custom_call" | custom-call | flops 10737418240 | bytes 11010048 | tf_op jit(solution)/shard_map/attend_back/pallas_call | solution.py:449
  99.4 1.0 copy-done.25
  100.9 6.9 %attend.2 = (bf16[1,256,1024]{2,1,0:T(8,128)(2,1)S(1)}, f32[1,16,256]{2,1,0:T(8,128)S(1)}) custom-call(s32[1]{0:T(128)} %bitcast.place_ref, s32[2]{0:T(128)S(1)} %copy-done.29, bf16[2,256,1024]{2,1,0:T(8,128)(2,1)S(1)} %copy-done.33, bf16[2,256,1024]{2,1,0:T(8,128)(2,1)S(1)} %copy-done.33, bf16[2,2,256,1024]{3,2,1,0:T(8,128)(2,1)} %get-tuple-element.43.rest_0_, ...), custom_call_target="tpu_custom_call" | custom-call | flops 4294967296 | bytes 5242880 | tf_op jit(solution)/shard_map/attend/pallas_call | solution.py:243
  107.9 0.8 copy-done.41
  108.7 20.9 %feed_forward.3 = (bf16[2,256,1024]{2,1,0:T(8,128)(2,1)}, f32[1,256,1024]{2,1,0:T(8,128)}, bf16[1,256,1024]{2,1,0:T(8,128)(2,1)}) custom-call(s32[1]{0:T(128)} %bitcast.place_ref, s32[2]{0:T(128)} %length_ref.11, s32[2]{0:T(128)} %source_ref.3, bf16[2,256,1024]{2,1,0:T(8,128)(2,1)} %tokens_ref.9, ...), custom_call_target="tpu_custom_call", output_to_operand_aliasing={{0}: (14, {})} | custom-call | flops 9663676416 | bytes 23068672 | tf_op jit(solution)/shard_map/feed_forward/pallas_call | solution.py:544
  129.6 1.0 copy-done.37
  130.6 1.3 prefix_back.2
  132.0 1.0 copy-done.35
  133.0 1.2 copy-done.38
  134.2 9.2 %attend_back.2 = (bf16[1,256,1024]{2,1,0:T(8,128)(2,1)S(1)}, bf16[1,2,256,1024]{3,2,1,0:T(8,128)(2,1)S(1)}, bf16[1,2,256,1024]{3,2,1,0:T(8,128)(2,1)S(1)}, bf16[...) custom-call(s32[1]{0:T(128)} %bitcast.place_ref, s32[2]{0:T(128)S(1)} %copy-done.30, ...), custom_call_target="tpu_custom_call" | custom-call | flops 10737418240 | bytes 11010048 | tf_op jit(solution)/shard_map/attend_back/pallas_call | solution.py:449
  143.4 1.0 copy-done.26
  145.0 0.5 collective-permute-start.11
  145.5 1.9 collective-permute-done.11
  147.5 16.5 %collective-permute-start.12 = (f32[2,16,1024]{2,1,0:T(8,128)S(1)}, f32[2,16,1024]{2,1,0:T(8,128)S(1)}, u32[]{:S(2)}, u32[]{:S(2)}) collective-permute-start(f32[2,16,1024]{2,1,0:T(8,128)S(1)} %add.19), channel_id=1, source_target_pairs={{0,16},{8,24},{16,0},{24,8},{1,17},{9,25},{17,1},{25,9},{2,18},{10... | collective-permute-start | bytes 393224 | tf_op jit(solution)/shard_map/ppermute | solution.py:771
  164.0 1.2 copy-done.12
  165.2 3.9 %up_back.3 = bf16[1,256,1024]{2,1,0:T(8,128)(2,1)S(1)} custom-call(bf16[1,2,256,1024]{3,2,1,0:T(8,128)(2,1)S(1)} %copy-done.12, bf16[1,2,256,1024]{3,2,1,0:T(8,128)(2,1)} %collective-permute-done.9.received_ref, bf16[1024,3072]{1,0:T(8,128)(2,1)S(1)} %bitcast.14), custom_call_target="tpu_custom_call" | custom-call | flops 1073741824 | bytes 6815744 | tf_op jit(solution)/shard_map/up_back/pallas_call | solution.py:613
  169.1 1.3 collective-permute-start.10
  170.4 1.6 collective-permute-start.13
  172.0 2.9 %up_back.2 = bf16[1,256,1024]{2,1,0:T(8,128)(2,1)S(1)} custom-call(bf16[1,2,256,1024]{3,2,1,0:T(8,128)(2,1)S(1)} %get-tuple-element.57.own_ref, bf16[1,2,256,1024]{3,2,1,0:T(8,128)(2,1)S(1)} %collective-permute-done.6.received_ref, bf16[1024,3072]{1,0:T(8,128)(2,1)S(1)} %bitcast.14), custom_call_target="tpu_custom_call" | custom-call | flops 1073741824 | bytes 6815744 | tf_op jit(solution)/shard_map/up_back/pallas_call | solution.py:613
  174.8 1.5 collective-permute-start.7
  176.4 1.6 collective-permute-start.14
  178.0 3.4 %collective-permute-done.14 = f32[2,16,1024]{2,1,0:T(8,128)S(1)} collective-permute-done((f32[2,16,1024]{2,1,0:T(8,128)S(1)}, f32[2,16,1024]{2,1,0:T(8,128)S(1)}, u32[]{:S(2)}, u32[]{:S(2)}) %collective-permute-start.14) | collective-permute-done | bytes 131104 | tf_op jit(solution)/shard_map/ppermute | solution.py:771
  181.5 2.6 %collective-permute-start.15 = (f32[2,16,1024]{2,1,0:T(8,128)S(1)}, f32[2,16,1024]{2,1,0:T(8,128)S(1)}, u32[]{:S(2)}, u32[]{:S(2)}) collective-permute-start(f32[2,16,1024]{2,1,0:T(8,128)S(1)} %add.22), channel_id=1, source_target_pairs={{0,4},{1,5},{2,6},{3,7},{4,0},{5,1},{6,2},{7,3},{8,12},{9,13},{10,... | collective-permute-start | bytes 393224 | tf_op jit(solution)/shard_map/ppermute | solution.py:771
  184.1 5.2 %collective-permute-done.15 = f32[2,16,1024]{2,1,0:T(8,128)S(1)} collective-permute-done((f32[2,16,1024]{2,1,0:T(8,128)S(1)}, f32[2,16,1024]{2,1,0:T(8,128)S(1)}, u32[]{:S(2)}, u32[]{:S(2)}) %collective-permute-start.15) | collective-permute-done | bytes 131104 | tf_op jit(solution)/shard_map/ppermute | solution.py:771
  189.4 4.5 %prefix_network_back.1 = (f32[10,1024]{1,0:T(8,128)}, f32[1024,512]{1,0:T(8,128)}, f32[1,512]{1,0:T(1,128)}, f32[512,2048]{1,0:T(8,128)}, f32[1,2048]{1,0:T(1,128)}) custom-call(f32[2,16,1024]{2,1,0:T(8,128)S(1)} %add.23.grad_ref, f32[10,1024]{1,0:T(8,128)S(1)} %convert_element_type.3.table_ref, bf16[1024,512]{1,0:T(8,128)(2,1)S(1)} %copy-done.6, ...), custom_call_target="tpu_custom_call" | custom-call | tf_op jit(solution)/shard_map/prefix_network_back/pallas_call | solution.py:749
  193.9 5.5 %project_back.2.rest_1_ = f32[2,256,1024]{2,1,0:T(8,128)} custom-call(bf16[2,256,1024]{2,1,0:T(8,128)(2,1)S(1)} %copy-done.4, f32[1,1024]{1,0:T(1,128)S(1)} %bitcast.18, f32[1,256,1024]{2,1,0:T(8,128)S(1)} %copy-done.7, bf16[1,256,1024]{2,1,0:T(8,128)(2,1)S(1)} %get-tuple-element.64.query_ref, bf16[1,2,256,1024]{3,2,1,0:T(8,128)(2,1)S(1)} %get-tuple-element.65.own_ref, ...), custom_call_target="tpu_custom_call" | custom-call | flops 1610612736 | bytes 11534336 | tf_op jit(solution)/shard_map/project_back/pallas_call | solution.py:673
  199.5 5.5 %project_back.3 = f32[2,256,1024]{2,1,0:T(8,128)} custom-call(bf16[2,256,1024]{2,1,0:T(8,128)(2,1)S(1)} %copy-done.4, f32[1,1024]{1,0:T(1,128)S(1)} %bitcast.19, f32[1,256,1024]{2,1,0:T(8,128)S(1)} %copy-done.8, bf16[1,256,1024]{2,1,0:T(8,128)(2,1)S(1)} %copy-done.15, bf16[1,2,256,1024]{3,2,1,0:T(8,128)(2,1)S(1)} %copy-done.10, ...), custom_call_target="tpu_custom_call", output_to_operand_aliasing={{}: (8, {})} | custom-call | flops 1610612736 | bytes 11534336 | tf_op jit(solution)/shard_map/project_back/pallas_call | solution.py:673
  (104 shorter events, 1.8 us)
Async XLA Ops:
  0.6 2.8 %copy-start = (bf16[1024,3072]{1,0:T(8,128)(2,1)S(1)}, bf16[1024,3072]{1,0:T(8,128)(2,1)}, u32[]{:S(2)}) copy-start(bf16[1024,3072]{1,0:T(8,128)(2,1)} %weight_ref.13) | copy-start | bytes 18874372
  6.7 24.8 %copy-start.1 = (bf16[1024,3072]{1,0:T(8,128)(2,1)S(1)}, bf16[1024,3072]{1,0:T(8,128)(2,1)}, u32[]{:S(2)}) copy-start(bf16[1024,3072]{1,0:T(8,128)(2,1)} %weight_ref.13) | copy-start | bytes 18874372
  13.6 21.3 %copy-start.31 = (bf16[2,256,1024]{2,1,0:T(8,128)(2,1)}, bf16[2,256,1024]{2,1,0:T(8,128)(2,1)S(1)}, u32[]{:S(2)}) copy-start(bf16[2,256,1024]{2,1,0:T(8,128)(2,1)S(1)} %get-tuple-element.42.query_all_ref.query_ref) | copy-start | bytes 3145732
  13.6 17.9 %copy-start.20 = (f32[3072]{0:T(1024)S(1)}, f32[3072]{0:T(1024)}, u32[]{:S(2)}) copy-start(f32[3072]{0:T(1024)} %param.28) | copy-start | bytes 36868
  13.6 44.5 %collective-permute-start = (bf16[2,2,256,1024]{3,2,1,0:T(8,128)(2,1)}, bf16[2,2,256,1024]{3,2,1,0:T(8,128)(2,1)}, u32[]{:S(2)}, u32[]{:S(2)}) collective-permute-start(bf16[2,2,256,1024]{3,2,1,0:T(8,128)(2,1)} %get-tuple-element.43.rest_0_), channel_id=1, source_target_pairs={{0,8},{8,0},{16,24},{24,16},{1,9},{9,1},{17,25},{25,17},{2,10},{10... | collective-permute-start | bytes 6291464 | tf_op jit(solution)/shard_map/ppermute | solution.py:793
  14.9 25.6 %copy-start.5 = (bf16[512,2048]{1,0:T(8,128)(2,1)S(1)}, bf16[512,2048]{1,0:T(8,128)(2,1)}, u32[]{:S(2)}) copy-start(bf16[512,2048]{1,0:T(8,128)(2,1)} %fan_ref.3) | copy-start | bytes 6291460
  14.9 25.6 %copy-start.6 = (bf16[1024,512]{1,0:T(8,128)(2,1)S(1)}, bf16[1024,512]{1,0:T(8,128)(2,1)}, u32[]{:S(2)}) copy-start(bf16[1024,512]{1,0:T(8,128)(2,1)} %lift_ref.3) | copy-start | bytes 3145732
  14.9 25.6 %copy-start.16 = (bf16[10,1024]{1,0:T(8,128)(2,1)S(1)}, bf16[10,1024]{1,0:T(8,128)(2,1)}, u32[]{:S(2)}) copy-start(bf16[10,1024]{1,0:T(8,128)(2,1)} %table_ref.1) | copy-start | bytes 61444
  14.9 25.6 %copy-start.23 = (f32[2048]{0:T(1024)S(1)}, f32[2048]{0:T(1024)}, u32[]{:S(2)}) copy-start(f32[2048]{0:T(1024)} %param.41) | copy-start | bytes 24580
  14.9 25.6 %copy-start.24 = (f32[512]{0:T(512)S(1)}, f32[512]{0:T(512)}, u32[]{:S(2)}) copy-start(f32[512]{0:T(512)} %param.39) | copy-start | bytes 6148
  15.0 16.5 %collective-permute-start.3 = (bf16[1,256,1024]{2,1,0:T(8,128)(2,1)S(1)}, bf16[1,256,1024]{2,1,0:T(8,128)(2,1)S(1)}, u32[]{:S(2)}, u32[]{:S(2)}) collective-permute-start(bf16[1,256,1024]{2,1,0:T(8,128)(2,1)S(1)} %get-tuple-element.77), channel_id=1, source_target_pairs={{0,16},{8,24},{1,17},{9,25},{2,18},{10,26},{3,19},{11,27},{4,20},{... | collective-permute-start | bytes 1572872 | tf_op jit(solution)/shard_map/ppermute | solution.py:789
  34.9 16.5 %copy-start.18 = (f32[1024]{0:T(1024)S(1)}, f32[1024]{0:T(1024)}, u32[]{:S(2)}) copy-start(f32[1024]{0:T(1024)} %param.25) | copy-start | bytes 12292
  34.9 16.5 %copy-start.22 = (f32[1024]{0:T(1024)S(1)}, f32[1024]{0:T(1024)}, u32[]{:S(2)}) copy-start(f32[1024]{0:T(1024)} %param.26) | copy-start | bytes 12292
  34.9 23.2 %collective-permute-start.4 = (bf16[1,2,256,1024]{3,2,1,0:T(8,128)(2,1)}, bf16[1,2,256,1024]{3,2,1,0:T(8,128)(2,1)}, u32[]{:S(2)}, u32[]{:S(2)}) collective-permute-start(bf16[1,2,256,1024]{3,2,1,0:T(8,128)(2,1)} %project_up.3.rest_2_), channel_id=1, source_target_pairs={{0,8},{8,0},{16,24},{24,16},{1,9},{9,1},{17,25},{25,17},{2,10},{10... | collective-permute-start | bytes 3145736 | tf_op jit(solution)/shard_map/ppermute | solution.py:803
  34.9 16.5 %collective-permute-start.1 = (bf16[1,256,1024]{2,1,0:T(8,128)(2,1)}, bf16[1,256,1024]{2,1,0:T(8,128)(2,1)}, u32[]{:S(2)}, u32[]{:S(2)}) collective-permute-start(bf16[1,256,1024]{2,1,0:T(8,128)(2,1)} %get-tuple-element.78), channel_id=1, source_target_pairs={{0,16},{8,24},{1,17},{9,25},{2,18},{10,26},{3,19},{11,27},{4,20},{... | collective-permute-start | bytes 1572872 | tf_op jit(solution)/shard_map/ppermute | solution.py:789
  51.5 2.8 %copy-start.2 = (bf16[1024,3072]{1,0:T(8,128)(2,1)S(1)}, bf16[1024,3072]{1,0:T(8,128)(2,1)}, u32[]{:S(2)}) copy-start(bf16[1024,3072]{1,0:T(8,128)(2,1)} %weight_ref.13) | copy-start | bytes 18874372
  54.3 3.9 %copy-start.28 = (s32[2]{0:T(128)S(1)}, s32[2]{0:T(128)}, u32[]{:S(2)}) copy-start(s32[2]{0:T(128)} %length_ref.11) | copy-start | bytes 28
  54.3 3.9 %copy-start.32 = (bf16[2,256,1024]{2,1,0:T(8,128)(2,1)S(1)}, bf16[2,256,1024]{2,1,0:T(8,128)(2,1)}, u32[]{:S(2)}) copy-start(bf16[2,256,1024]{2,1,0:T(8,128)(2,1)} %copy-done.31) | copy-start | bytes 3145732
  58.0 42.9 %copy-start.13 = (bf16[1,2,256,1024]{3,2,1,0:T(8,128)(2,1)}, bf16[1,2,256,1024]{3,2,1,0:T(8,128)(2,1)S(1)}, u32[]{:S(2)}) copy-start(bf16[1,2,256,1024]{3,2,1,0:T(8,128)(2,1)S(1)} %project_up.2.rest_2_) | copy-start | bytes 3145732
  58.0 42.8 %collective-permute-start.2 = (bf16[1,2,256,1024]{3,2,1,0:T(8,128)(2,1)S(1)}, bf16[1,2,256,1024]{3,2,1,0:T(8,128)(2,1)S(1)}, u32[]{:S(2)}, u32[]{:S(2)}) collective-permute-start(bf16[1,2,256,1024]{3,2,1,0:T(8,128)(2,1)S(1)} %project_up.2.rest_2_), channel_id=1, source_target_pairs={{0,8},{8,0},{16,24},{24,16},{1,9},{9,1},{17,25},{25,17},{2,10},{10... | collective-permute-start | bytes 3145736 | tf_op jit(solution)/shard_map/ppermute | solution.py:803
  65.8 20.9 %copy-start.44 = (bf16[1,256,1024]{2,1,0:T(8,128)(2,1)S(1)}, bf16[1,256,1024]{2,1,0:T(8,128)(2,1)}, u32[]{:S(2)}) copy-start(bf16[1,256,1024]{2,1,0:T(8,128)(2,1)} %copy-done.43) | copy-start | bytes 1572868
  86.7 3.4 %copy-start.29 = (s32[2]{0:T(128)S(1)}, s32[2]{0:T(128)}, u32[]{:S(2)}) copy-start(s32[2]{0:T(128)} %length_ref.11) | copy-start | bytes 28
  90.1 10.8 %copy-start.33 = (bf16[2,256,1024]{2,1,0:T(8,128)(2,1)S(1)}, bf16[2,256,1024]{2,1,0:T(8,128)(2,1)}, u32[]{:S(2)}) copy-start(bf16[2,256,1024]{2,1,0:T(8,128)(2,1)} %copy-done.31) | copy-start | bytes 3145732
  100.4 7.4 %copy-start.11 = (bf16[1,2,256,1024]{3,2,1,0:T(8,128)(2,1)}, bf16[1,2,256,1024]{3,2,1,0:T(8,128)(2,1)S(1)}, u32[]{:S(2)}) copy-start(bf16[1,2,256,1024]{3,2,1,0:T(8,128)(2,1)S(1)} %get-tuple-element.67.own_ref) | copy-start | bytes 3145732
  100.4 63.5 %collective-permute-start.9 = (bf16[1,2,256,1024]{3,2,1,0:T(8,128)(2,1)}, bf16[1,2,256,1024]{3,2,1,0:T(8,128)(2,1)}, u32[]{:S(2)}, u32[]{:S(2)}) collective-permute-start(bf16[1,2,256,1024]{3,2,1,0:T(8,128)(2,1)} %get-tuple-element.68), channel_id=1, source_target_pairs={{0,8},{8,0},{16,24},{24,16},{1,9},{9,1},{17,25},{25,17},{2,10},{10... | collective-permute-start | bytes 3145736 | tf_op jit(solution)/shard_map/ppermute | solution.py:816
  100.9 7.0 %copy-start.27 = (bf16[1,2,256,1024]{3,2,1,0:T(8,128)(2,1)}, bf16[1,2,256,1024]{3,2,1,0:T(8,128)(2,1)S(1)}, u32[]{:S(2)}) copy-start(bf16[1,2,256,1024]{3,2,1,0:T(8,128)(2,1)S(1)} %collective-permute-done.2.rest_3_) | copy-start | bytes 3145732
  108.7 20.9 %copy-start.34 = (bf16[2,256,1024]{2,1,0:T(8,128)(2,1)S(1)}, bf16[2,256,1024]{2,1,0:T(8,128)(2,1)}, u32[]{:S(2)}) copy-start(bf16[2,256,1024]{2,1,0:T(8,128)(2,1)} %copy-done.31) | copy-start | bytes 3145732
  108.7 20.9 %copy-start.42 = (bf16[1,256,1024]{2,1,0:T(8,128)(2,1)S(1)}, bf16[1,256,1024]{2,1,0:T(8,128)(2,1)}, u32[]{:S(2)}) copy-start(bf16[1,256,1024]{2,1,0:T(8,128)(2,1)} %copy-done.41) | copy-start | bytes 1572868
  129.6 3.4 %copy-start.30 = (s32[2]{0:T(128)S(1)}, s32[2]{0:T(128)}, u32[]{:S(2)}) copy-start(s32[2]{0:T(128)} %length_ref.11) | copy-start | bytes 28
  133.0 31.0 %slice-start = ((s8[6291456]{0:T(1024)(128)(4,1)}), s8[4194304]{0:T(1024)(128)(4,1)S(1)}, s32[]{:S(2)}) async-start(s8[6291456]{0:T(1024)(128)(4,1)} %bitcast.13), calls=%async_computation | async-start | bytes 8388608
  134.2 29.8 %slice-start.1 = ((s8[6291456]{0:T(1024)(128)(4,1)}), s8[2097152]{0:T(1024)(128)(4,1)S(1)}, s32[]{:S(2)}) async-start(s8[6291456]{0:T(1024)(128)(4,1)} %bitcast.13), calls=%async_computation.1 | async-start | bytes 4194304
  144.4 24.7 %copy-start.9 = (bf16[1,2,256,1024]{3,2,1,0:T(8,128)(2,1)}, bf16[1,2,256,1024]{3,2,1,0:T(8,128)(2,1)S(1)}, u32[]{:S(2)}) copy-start(bf16[1,2,256,1024]{3,2,1,0:T(8,128)(2,1)S(1)} %get-tuple-element.55.own_ref) | copy-start | bytes 3145732
  144.4 24.7 %copy-start.14 = (bf16[1,256,1024]{2,1,0:T(8,128)(2,1)}, bf16[1,256,1024]{2,1,0:T(8,128)(2,1)S(1)}, u32[]{:S(2)}) copy-start(bf16[1,256,1024]{2,1,0:T(8,128)(2,1)S(1)} %get-tuple-element.54.query_ref) | copy-start | bytes 1572868
  144.4 27.6 %collective-permute-start.6 = (bf16[1,2,256,1024]{3,2,1,0:T(8,128)(2,1)}, bf16[1,2,256,1024]{3,2,1,0:T(8,128)(2,1)S(1)}, u32[]{:S(2)}, u32[]{:S(2)}) collective-permute-start(bf16[1,2,256,1024]{3,2,1,0:T(8,128)(2,1)} %get-tuple-element.58), channel_id=1, source_target_pairs={{0,8},{8,0},{16,24},{24,16},{1,9},{9,1},{17,25},{25,17},{2,10},{10... | collective-permute-start | bytes 3145736 | tf_op jit(solution)/shard_map/ppermute | solution.py:816
  144.4 49.4 %collective-permute-start.8 = (bf16[1,2,256,1024]{3,2,1,0:T(8,128)(2,1)}, bf16[1,2,256,1024]{3,2,1,0:T(8,128)(2,1)S(1)}, u32[]{:S(2)}, u32[]{:S(2)}) collective-permute-start(bf16[1,2,256,1024]{3,2,1,0:T(8,128)(2,1)} %copy-done.25), channel_id=1, source_target_pairs={{0,8},{8,0},{16,24},{24,16},{1,9},{9,1},{17,25},{25,17},{2,10},{10... | collective-permute-start | bytes 3145736 | tf_op jit(solution)/shard_map/ppermute | solution.py:813
  144.9 54.5 %collective-permute-start.5 = (bf16[1,2,256,1024]{3,2,1,0:T(8,128)(2,1)}, bf16[1,2,256,1024]{3,2,1,0:T(8,128)(2,1)S(1)}, u32[]{:S(2)}, u32[]{:S(2)}) collective-permute-start(bf16[1,2,256,1024]{3,2,1,0:T(8,128)(2,1)} %copy-done.26), channel_id=1, source_target_pairs={{0,8},{8,0},{16,24},{24,16},{1,9},{9,1},{17,25},{25,17},{2,10},{10... | collective-permute-start | bytes 3145736 | tf_op jit(solution)/shard_map/ppermute | solution.py:813
  145.0 2.5 %collective-permute-start.11 = (f32[2,16,1024]{2,1,0:T(8,128)S(1)}, f32[2,16,1024]{2,1,0:T(8,128)S(1)}, u32[]{:S(2)}, u32[]{:S(2)}) collective-permute-start(f32[2,16,1024]{2,1,0:T(8,128)S(1)} %add.18), channel_id=1, source_target_pairs={{0,8},{8,0},{16,24},{24,16},{1,9},{9,1},{17,25},{25,17},{2,10},{10... | collective-permute-start | bytes 393224 | tf_op jit(solution)/shard_map/ppermute | solution.py:771
  147.5 22.9 %collective-permute-start.12 = (f32[2,16,1024]{2,1,0:T(8,128)S(1)}, f32[2,16,1024]{2,1,0:T(8,128)S(1)}, u32[]{:S(2)}, u32[]{:S(2)}) collective-permute-start(f32[2,16,1024]{2,1,0:T(8,128)S(1)} %add.19), channel_id=1, source_target_pairs={{0,16},{8,24},{16,0},{24,8},{1,17},{9,25},{17,1},{25,9},{2,18},{10... | collective-permute-start | bytes 393224 | tf_op jit(solution)/shard_map/ppermute | solution.py:771
  169.1 24.8 %collective-permute-start.10 = (bf16[1,256,1024]{2,1,0:T(8,128)(2,1)S(1)}, bf16[1,256,1024]{2,1,0:T(8,128)(2,1)S(1)}, u32[]{:S(2)}, u32[]{:S(2)}) collective-permute-start(bf16[1,256,1024]{2,1,0:T(8,128)(2,1)S(1)} %up_back.3), channel_id=1, source_target_pairs={{16,0},{24,8},{17,1},{25,9},{18,2},{26,10},{19,3},{27,11},{20,4},{... | collective-permute-start | bytes 1572872 | tf_op jit(solution)/shard_map/ppermute | solution.py:818
  170.4 5.9 %collective-permute-start.13 = (f32[2,16,1024]{2,1,0:T(8,128)S(1)}, f32[2,16,1024]{2,1,0:T(8,128)S(1)}, u32[]{:S(2)}, u32[]{:S(2)}) collective-permute-start(f32[2,16,1024]{2,1,0:T(8,128)S(1)} %add.20), channel_id=1, source_target_pairs={{0,1},{1,0},{2,3},{3,2},{4,5},{5,4},{6,7},{7,6},{8,9},{9,8},{10,11... | collective-permute-start | bytes 393224 | tf_op jit(solution)/shard_map/ppermute | solution.py:771
  174.8 24.6 %collective-permute-start.7 = (bf16[1,256,1024]{2,1,0:T(8,128)(2,1)S(1)}, bf16[1,256,1024]{2,1,0:T(8,128)(2,1)S(1)}, u32[]{:S(2)}, u32[]{:S(2)}) collective-permute-start(bf16[1,256,1024]{2,1,0:T(8,128)(2,1)S(1)} %up_back.2), channel_id=1, source_target_pairs={{16,0},{24,8},{17,1},{25,9},{18,2},{26,10},{19,3},{27,11},{20,4},{... | collective-permute-start | bytes 1572872 | tf_op jit(solution)/shard_map/ppermute | solution.py:818
  176.4 17.5 %copy-start.4 = (bf16[2,256,1024]{2,1,0:T(8,128)(2,1)S(1)}, bf16[2,256,1024]{2,1,0:T(8,128)(2,1)}, u32[]{:S(2)}) copy-start(bf16[2,256,1024]{2,1,0:T(8,128)(2,1)} %tokens_ref.9) | copy-start | bytes 3145732
  176.4 17.5 %copy-start.7 = (f32[1,256,1024]{2,1,0:T(8,128)S(1)}, f32[1,256,1024]{2,1,0:T(8,128)}, u32[]{:S(2)}) copy-start(f32[1,256,1024]{2,1,0:T(8,128)} %get-tuple-element.59.residual_ref) | copy-start | bytes 3145732
  176.4 5.0 %collective-permute-start.14 = (f32[2,16,1024]{2,1,0:T(8,128)S(1)}, f32[2,16,1024]{2,1,0:T(8,128)S(1)}, u32[]{:S(2)}, u32[]{:S(2)}) collective-permute-start(f32[2,16,1024]{2,1,0:T(8,128)S(1)} %add.21), channel_id=1, source_target_pairs={{0,2},{1,3},{2,0},{3,1},{4,6},{5,7},{6,4},{7,5},{8,10},{9,11},{10,... | collective-permute-start | bytes 393224 | tf_op jit(solution)/shard_map/ppermute | solution.py:771
  181.5 7.9 %collective-permute-start.15 = (f32[2,16,1024]{2,1,0:T(8,128)S(1)}, f32[2,16,1024]{2,1,0:T(8,128)S(1)}, u32[]{:S(2)}, u32[]{:S(2)}) collective-permute-start(f32[2,16,1024]{2,1,0:T(8,128)S(1)} %add.22), channel_id=1, source_target_pairs={{0,4},{1,5},{2,6},{3,7},{4,0},{5,1},{6,2},{7,3},{8,12},{9,13},{10,... | collective-permute-start | bytes 393224 | tf_op jit(solution)/shard_map/ppermute | solution.py:771
  193.9 5.5 %copy-start.8 = (f32[1,256,1024]{2,1,0:T(8,128)S(1)}, f32[1,256,1024]{2,1,0:T(8,128)}, u32[]{:S(2)}) copy-start(f32[1,256,1024]{2,1,0:T(8,128)} %get-tuple-element.49.residual_ref) | copy-start | bytes 3145732
  193.9 5.5 %copy-start.10 = (bf16[1,2,256,1024]{3,2,1,0:T(8,128)(2,1)S(1)}, bf16[1,2,256,1024]{3,2,1,0:T(8,128)(2,1)}, u32[]{:S(2)}) copy-start(bf16[1,2,256,1024]{3,2,1,0:T(8,128)(2,1)} %copy-done.9) | copy-start | bytes 3145732
  193.9 5.5 %copy-start.15 = (bf16[1,256,1024]{2,1,0:T(8,128)(2,1)S(1)}, bf16[1,256,1024]{2,1,0:T(8,128)(2,1)}, u32[]{:S(2)}) copy-start(bf16[1,256,1024]{2,1,0:T(8,128)(2,1)} %copy-done.14) | copy-start | bytes 1572868
  (15 other events, 15.7 us)
